TPU v7x, 768 devices: a whole 4x8x12 slice. The times are simulated.
768 devices in a mesh: section: 96 (over z, y), head: 8 (over x, core).
Axes of the slice: x: 4, y: 8, z: 12, core: 2. Of those that a mesh axis runs over, the one named last changes fastest.
Arguments:
- queries: bfloat16 [24576, 8192], P('section', 'head'), may hold values from -40 to 40
- new_keys: bfloat16 [24576, 1024], P('section', 'head'), may hold values from -6 to 6
- new_values: bfloat16 [24576, 1024], P('section', 'head'), may hold values from -6 to 6
- cache_keys: bfloat16 [96, 8, 768, 128], P('section', 'head'), may hold values from -6 to 6
- cache_values: bfloat16 [96, 8, 768, 128], P('section', 'head'), may hold values from -6 to 6
- key_counts: int32 [96], replicated, may hold values from 1 to 768, 36864 in all
- scale_exps: int32 [96, 2], replicated, may hold values from -2 to 2
- out_weight: bfloat16 [8192, 4096], P('head'), may hold values from -0.0625 to 0.0625
Outputs:
- handed: float32 [24576, 4096], P(('section', 'head'))
Inputs may be any that keep to these rules, and one draw needn't show every extreme that they name: `key_counts`: some section holds exactly 768 live slots, and the counts sum to 36864.
All inputs are finite; a program needn't handle non-finite values.
Results may differ from a plain program's by a relative error of at most 0.023.
Values may be sent and summed in bfloat16 or wider, within the bound.
No kernel may reach another device: no remote copies, remote signals or barrier semaphores. Data moves between devices by JAX's collectives and lax.ppermute only.
A program may use at most 64 MiB of HBM per device.

v0:
```python
import math

import jax
import jax.numpy as jnp
from jax import lax
from jax.sharding import PartitionSpec as P

HD = 128
GROUP = 8


def shifted(value, axis, steps):
    count = lax.axis_size(axis)
    first, last = (max(0, -steps), min(count, count - steps))
    return lax.ppermute(value, axis, [(source, source + steps) for source in range(first, last)])


def in_blocks(value, dim, size):
    dims = value.shape
    pieces = value.reshape(*dims[:dim], size, dims[dim] // size, *dims[dim + 1 :])
    return jnp.moveaxis(pieces, dim, 0)


def sum_at_owner(value, axis, dim):
    size = lax.axis_size(axis)
    pieces = lax.all_to_all(in_blocks(value, dim, size), axis, 0, 0, tiled=True)
    return jnp.sum(pieces.astype(jnp.float32), axis=0)


def shifted_2(value, axis, by):
    size = lax.axis_size(axis)
    return lax.ppermute(value, axis, [(i, (i + by) % size) for i in range(size)])


def partial_block(query_heads, key_block, value_block, visible, key_scale, value_scale):
    scores = jnp.einsum(
        "rkgh,kch->rkgc", query_heads, key_block, preferred_element_type=jnp.float32
    )
    scores = scores * (key_scale / math.sqrt(query_heads.shape[-1]))
    scores = jnp.where(visible, scores, -1e30)
    row_peak = jnp.max(scores, axis=-1)
    weights = jnp.where(visible, jnp.exp(scores - row_peak[..., None]), 0.0)
    row_total = jnp.sum(weights, axis=-1)
    summed = (
        jnp.einsum(
            "rkgc,kch->rkgh",
            weights.astype(jnp.bfloat16),
            value_block,
            preferred_element_type=jnp.float32,
        )
        * value_scale
    )
    return (summed.astype(jnp.bfloat16), row_peak, row_total)


def merge_blocks(pieces):
    peaks = jnp.stack([piece[1] for piece in pieces])
    top_peak = jnp.max(peaks, axis=0)
    factors = jnp.exp(peaks - top_peak[None])
    numer = sum(
        (factors[n][..., None] * pieces[n][0].astype(jnp.float32) for n in range(len(pieces)))
    )
    denom = sum((factors[n] * pieces[n][2] for n in range(len(pieces))))
    return numer / denom[..., None]


def on_device(
    queries, new_keys, new_values, cache_keys, cache_values, key_counts, scale_exps, out_weight
):
    rows = queries.shape[0]
    kv_local = cache_keys.shape[1]
    query_heads = queries.reshape(rows, kv_local, GROUP, HD)
    section_pos = lax.axis_index("section")
    positions = jnp.arange(rows, dtype=jnp.int32)
    causal = (positions[:, None] >= positions[None, :])[:, None, None, :]
    fresh_keys = new_keys.reshape(rows, kv_local, HD).transpose(1, 0, 2)
    fresh_values = new_values.reshape(rows, kv_local, HD).transpose(1, 0, 2)
    own_keys = cache_keys[0]
    own_values = cache_values[0]
    slots = jnp.arange(own_keys.shape[1], dtype=jnp.int32)

    def cache_terms(index):
        source = jnp.maximum(index, 0)
        visible = ((slots < key_counts[source]) & (index >= 0))[None, None, None, :]
        key_scale = jnp.exp2(scale_exps[source, 0].astype(jnp.float32))
        value_scale = jnp.exp2(scale_exps[source, 1].astype(jnp.float32))
        return (visible, key_scale, value_scale)

    own_terms = cache_terms(section_pos)
    pieces = [partial_block(query_heads, fresh_keys, fresh_values, causal, 1.0, 1.0)]
    pieces.append(partial_block(query_heads, own_keys, own_values, *own_terms))
    for distance in (1, 2):
        far_keys, far_values = shifted((cache_keys, cache_values), "section", distance)
        pieces.append(
            partial_block(
                query_heads, far_keys[0], far_values[0], *cache_terms(section_pos - distance)
            )
        )
    attended = merge_blocks(pieces).astype(jnp.bfloat16).reshape(rows, -1)
    projected = sum_at_owner(
        jnp.dot(attended, out_weight, preferred_element_type=jnp.float32).astype(jnp.bfloat16),
        "head",
        0,
    )
    return shifted_2(projected.astype(jnp.bfloat16), "section", 1).astype(projected.dtype)


def solution(mesh):
    in_specs = (
        P("section", "head"),
        P("section", "head"),
        P("section", "head"),
        P("section", "head", None, None),
        P("section", "head", None, None),
        P(),
        P(),
        P("head", None),
    )
    out_specs = P(("section", "head"), None)
    return jax.shard_map(
        on_device, mesh=mesh, in_specs=in_specs, out_specs=out_specs, check_vma=False
    )
```

profile of v0, /device:TPU:1, one launch (start us, length us, event | category | flops | bytes accessed | tf_op | source)
XLA Modules:
  0.0 93.1 jit_solution(9176509656369643720)
XLA Ops:
  0.0 0.0 copy-start
  0.0 0.0 copy-start.2
  0.0 4.2 %collective-permute-start = (bf16[1,1,768,128]{3,2,1,0:T(8,128)(2,1)}, bf16[1,1,768,128]{3,2,1,0:T(8,128)(2,1)S(1)}, u32[]{:S(2)}, u32[]{:S(2)}) collective-permute-start(bf16[1,1,768,128]{3,2,1,0:T(8,128)(2,1)} %param.11), channel_id=1, source_target_pairs={{0,8},{8,16},{16,24},{24,32},{32,40},{40,48},{48,56},{56,64},{64,7... | collective-permute-start | bytes 589832 | tf_op jit(solution)/shard_map/ppermute | solution.py:15
  4.2 4.2 %collective-permute-start.1 = (bf16[1,1,768,128]{3,2,1,0:T(8,128)(2,1)}, bf16[1,1,768,128]{3,2,1,0:T(8,128)(2,1)S(1)}, u32[]{:S(2)}, u32[]{:S(2)}) collective-permute-start(bf16[1,1,768,128]{3,2,1,0:T(8,128)(2,1)} %param.11), channel_id=1, source_target_pairs={{0,16},{8,24},{16,32},{24,40},{32,48},{40,56},{48,64},{56,72},{64,... | collective-permute-start | bytes 589832 | tf_op jit(solution)/shard_map/ppermute | solution.py:15
  8.4 1.1 %copy.17 = bf16[1,1,768,128]{2,3,1,0:T(8,128)(2,1)S(1)} copy(bf16[1,1,768,128]{3,2,1,0:T(8,128)(2,1)} %param.12) | data formatting | bytes 393216 | tf_op args[4]
  9.5 4.4 %collective-permute-start.2 = (bf16[1,1,768,128]{2,3,1,0:T(8,128)(2,1)S(1)}, bf16[1,1,768,128]{2,3,1,0:T(8,128)(2,1)S(1)}, u32[]{:S(2)}, u32[]{:S(2)}) collective-permute-start(bf16[1,1,768,128]{2,3,1,0:T(8,128)(2,1)S(1)} %copy.17), channel_id=1, source_target_pairs={{0,8},{8,16},{16,24},{24,32},{32,40},{40,48},{48,56},{56,64},{64,7... | collective-permute-start | bytes 589832 | tf_op jit(solution)/shard_map/ppermute | solution.py:15
  13.9 2.4 %collective-permute-start.3 = (bf16[1,1,768,128]{2,3,1,0:T(8,128)(2,1)S(1)}, bf16[1,1,768,128]{2,3,1,0:T(8,128)(2,1)S(1)}, u32[]{:S(2)}, u32[]{:S(2)}) collective-permute-start(bf16[1,1,768,128]{2,3,1,0:T(8,128)(2,1)S(1)} %copy.17), channel_id=1, source_target_pairs={{0,16},{8,24},{16,32},{24,40},{32,48},{40,56},{48,64},{56,72},{64,... | collective-permute-start | bytes 589832 | tf_op jit(solution)/shard_map/ppermute | solution.py:15
  16.4 1.4 %fusion.129 = (s32[1]{0:T(128)}, s32[1]{0:T(128)}, s32[1]{0:T(128)}) fusion(s32[96]{0:T(128)} %param.13, s32[]{:T(128)S(6)} %max.9, s32[]{:T(128)S(6)} %max.11, s32[]{:T(128)S(6)} %max.10), kind=kLoop, calls=%fused_computation.118 | loop fusion | bytes 36 | tf_op jit(solution)/shard_map/dynamic_slice | solution.py:84
  17.8 1.6 %constant_dynamic-slice_fusion.2 = (s32[1,1]{0,1:T(1,128)}, s32[1,1]{0,1:T(1,128)}, s32[1,1]{0,1:T(1,128)}, s32[1,1]{0,1:T(1,128)}, s32[1,1]{0,1:T(1,128)}, /*index=5*/s32[1,1]{0,1:T(1,128)}) fusion(s32[96,2]{0,1:T(2,128)} %param.14, s32[]{:T(128)S(6)} %max.9, s32[]{:T(128)S(6)} %max.11, s32[]{:T(128)S(6)} %max.10), kind=kLoop, calls=%fused_computation.105 | loop fusion | bytes 60 | tf_op jit(solution)/shard_map/dynamic_slice | solution.py:86
  23.4 0.6 fusion.118
  24.1 0.6 fusion.119
  24.6 0.7 fusion.117
  25.3 0.0 copy-done
  25.3 1.9 %bitcast_reduce_fusion.2 = (f32[256,8]{0,1:T(8,128)S(1)}, f32[768,256,8]{1,0,2:T(8,128)S(1)}) fusion(f32[]{:T(128)} %bitcast.7, pred[768]{0:T(1024)(128)(4,1)S(1)} %fusion.117, bf16[1,1,768,128]{3,2,1,0:T(8,128)(2,1)} %param.11, bf16[256,1024]{1,0:T(8,128)(2,1)S(1)} %copy-done), kind=kOutput, calls=%fused_computation.11 | convolution fusion | flops 407369728 | bytes 7021316 | tf_op jit(solution)/shard_map/rkgh,kch->rkgc/dot_general | solution.py:36
  27.3 0.0 copy-done.2
  27.3 0.5 fusion.27
  27.8 2.0 %fusion.6 = f32[256,8]{0,1:T(8,128)S(1)} fusion(f32[768,256,8]{1,0,2:T(8,128)S(1)} %get-tuple-element.23, f32[256,8]{0,1:T(8,128)S(1)} %get-tuple-element.22, f32[]{:T(128)} %bitcast.7, pred[768]{0:T(1024)(128)(4,1)S(1)} %fusion.117), kind=kLoop, calls=%fused_computation.16 | loop fusion | flops 7862272 | bytes 6308612 | tf_op jit(solution)/shard_map/reduce_sum | solution.py:43
  29.8 0.5 fusion.28
  30.3 0.0 collective-permute-done
  30.3 1.0 %bitcast_reduce_fusion.1 = (f32[256,8]{0,1:T(8,128)S(1)}, f32[768,256,8]{1,0,2:T(8,128)S(1)}) fusion(f32[]{:T(128)} %bitcast.14, pred[768]{0:T(1024)(128)(4,1)S(1)} %fusion.118, bf16[1,1,768,128]{3,2,1,0:T(8,128)(2,1)S(1)} %collective-permute-done, bf16[256,1024]{1,0:T(8,128)(2,1)S(1)} %copy-done), kind=kOutput, calls=%fused_computation.6 | convolution fusion | flops 407369728 | bytes 7021316 | tf_op jit(solution)/shard_map/rkgh,kch->rkgc/dot_general | solution.py:36
  31.3 0.0 collective-permute-done.1
  31.4 1.0 %bitcast_reduce_fusion = (f32[256,8]{0,1:T(8,128)S(1)}, f32[768,256,8]{1,0,2:T(8,128)S(1)}) fusion(f32[]{:T(128)} %bitcast.21, pred[768]{0:T(1024)(128)(4,1)S(1)} %fusion.119, bf16[1,1,768,128]{3,2,1,0:T(8,128)(2,1)S(1)} %collective-permute-done.1, bf16[256,1024]{1,0:T(8,128)(2,1)S(1)} %copy-done), kind=kOutput, calls=%fused_computation.1 | convolution fusion | flops 407369728 | bytes 7021316 | tf_op jit(solution)/shard_map/rkgh,kch->rkgc/dot_general | solution.py:36
  32.4 0.0 copy-start.3
  32.4 2.0 %fusion.8 = f32[256,8]{0,1:T(8,128)S(1)} fusion(f32[768,256,8]{1,0,2:T(8,128)S(1)} %get-tuple-element.21, f32[256,8]{0,1:T(8,128)S(1)} %get-tuple-element.20, f32[]{:T(128)} %bitcast.14, pred[768]{0:T(1024)(128)(4,1)S(1)} %fusion.118), kind=kLoop, calls=%fused_computation.18 | loop fusion | flops 7862272 | bytes 6308612 | tf_op jit(solution)/shard_map/reduce_sum | solution.py:43
  34.4 2.2 %fusion.10 = f32[256,8]{0,1:T(8,128)S(1)} fusion(f32[768,256,8]{1,0,2:T(8,128)S(1)} %get-tuple-element.19, f32[256,8]{0,1:T(8,128)S(1)} %get-tuple-element.18, f32[]{:T(128)} %bitcast.21, pred[768]{0:T(1024)(128)(4,1)S(1)} %fusion.119), kind=kLoop, calls=%fused_computation.20 | loop fusion | flops 7862272 | bytes 6308612 | tf_op jit(solution)/shard_map/reduce_sum | solution.py:43
  36.7 0.0 copy-done.3
  36.7 0.7 fusion.86
  37.4 0.0 collective-permute-done.2
  37.4 1.7 %fusion.69 = f32[1,128,256,8]{2,1,3,0:T(8,128)S(1)} fusion(f32[768,256,8]{1,0,2:T(8,128)S(1)} %get-tuple-element.21, f32[256,8]{0,1:T(8,128)S(1)} %get-tuple-element.20, f32[]{:T(128)} %bitcast.14, pred[768]{0:T(1024)(128)(4,1)S(1)} %fusion.118, f32[]{:T(128)} %bitcast.41, f32[256,8]{0,1:T(8,128)S(1)} %get-tuple-element.7, ...), kind=kOutput, calls=%fused_computation.52 | convolution fusion | flops 411566080 | bytes 7553800 | tf_op jit(solution)/shard_map/rkgc,kch->rkgh/dot_general | solution.py:45
  39.1 0.0 copy-start.1
  39.1 0.0 collective-permute-done.3
  39.1 0.0 slice-start
  39.2 1.7 %fusion.81 = f32[1,128,256,8]{2,1,3,0:T(8,128)S(1)} fusion(f32[768,256,8]{1,0,2:T(8,128)S(1)} %get-tuple-element.19, f32[256,8]{0,1:T(8,128)S(1)} %get-tuple-element.18, f32[]{:T(128)} %bitcast.21, pred[768]{0:T(1024)(128)(4,1)S(1)} %fusion.119, f32[]{:T(128)} %bitcast.48, f32[256,8]{0,1:T(8,128)S(1)} %get-tuple-element.6, ...), kind=kOutput, calls=%fused_computation.56 | convolution fusion | flops 411566080 | bytes 7553800 | tf_op jit(solution)/shard_map/rkgc,kch->rkgh/dot_general | solution.py:45
  40.9 0.0 copy-done.1
  40.9 0.0 slice-start.1
  40.9 1.8 %divide_convert_fusion = bf16[1,128,256,8]{2,1,3,0:T(8,128)(2,1)S(1)} fusion(f32[1,128,256,8]{2,1,3,0:T(8,128)S(1)} %fusion.81, f32[1,128,256,8]{2,1,3,0:T(8,128)S(1)} %fusion.69, f32[1,128,256,8]{2,1,3,0:T(8,128)S(1)} %fusion.86, f32[768,256,8]{1,0,2:T(8,128)S(1)} %get-tuple-element.23, f32[256,8]{0,1:T(8,128)S(1)} %get-tuple-element.22, f32[]{:T(128)} %bitcast.7, ...), kind=kOutput, calls=%fused_computation.62 | convolution fusion | flops 412876800 | bytes 10183432 | tf_op jit(solution)/shard_map/rkgc,kch->rkgh/dot_general | solution.py:45
  42.7 0.0 slice-done
  42.7 0.5 slice-done.1
  43.2 2.5 %convolution_convert_fusion = bf16[256,4096]{1,0:T(8,128)(2,1)S(1)} fusion(bf16[256,1024]{0,1:T(8,128)(2,1)S(1)} %bitcast.366, bf16[1024,4096]{1,0:T(8,128)(2,1)S(1)} %bitcast.364), kind=kOutput, calls=%fused_computation.15 | convolution fusion | flops 2148532224 | bytes 11010048 | tf_op jit(solution)/shard_map/dot_general | solution.py:101
  45.8 32.0 %all_to_all.5 = bf16[8,32,4096]{2,1,0:T(8,128)(2,1)S(1)} all-to-all(bf16[8,32,4096]{2,1,0:T(8,128)(2,1)S(1)} %bitcast.365), channel_id=1, replica_groups=mesh['section'=96,'head'=8] {'head'}, dimensions={0} | all-to-all | bytes 4194304 | tf_op jit(solution)/shard_map/all_to_all | solution.py:26
  77.8 0.3 reduce_sum.52
  78.2 2.3 %collective-permute-start.4 = (bf16[32,4096]{1,0:T(8,128)(2,1)S(1)}, bf16[32,4096]{1,0:T(8,128)(2,1)S(1)}, u32[]{:S(2)}, u32[]{:S(2)}) collective-permute-start(bf16[32,4096]{1,0:T(8,128)(2,1)S(1)} %reduce_sum.52), channel_id=1, source_target_pairs={{0,8},{8,16},{16,24},{24,32},{32,40},{40,48},{48,56},{56,64},{64,7... | collective-permute-start | bytes 786440 | tf_op jit(solution)/shard_map/ppermute | solution.py:32
  80.5 11.8 %collective-permute-done.4 = bf16[32,4096]{1,0:T(8,128)(2,1)S(1)} collective-permute-done((bf16[32,4096]{1,0:T(8,128)(2,1)S(1)}, bf16[32,4096]{1,0:T(8,128)(2,1)S(1)}, u32[]{:S(2)}, u32[]{:S(2)}) %collective-permute-start.4) | collective-permute-done | bytes 262176 | tf_op jit(solution)/shard_map/ppermute | solution.py:32
  92.3 0.8 convert_element_type.136
  (6 shorter events, 0.1 us)
Async XLA Ops:
  0.0 25.3 %copy-start = (bf16[256,1024]{1,0:T(8,128)(2,1)S(1)}, bf16[256,1024]{1,0:T(8,128)(2,1)}, u32[]{:S(2)}) copy-start(bf16[256,1024]{1,0:T(8,128)(2,1)} %param.8) | copy-start | bytes 1572868
  0.0 27.3 %copy-start.2 = (bf16[256,128]{1,0:T(8,128)(2,1)S(1)}, bf16[256,128]{1,0:T(8,128)(2,1)}, u32[]{:S(2)}) copy-start(bf16[256,128]{1,0:T(8,128)(2,1)} %param.9) | copy-start | bytes 196612
  0.0 30.3 %collective-permute-start = (bf16[1,1,768,128]{3,2,1,0:T(8,128)(2,1)}, bf16[1,1,768,128]{3,2,1,0:T(8,128)(2,1)S(1)}, u32[]{:S(2)}, u32[]{:S(2)}) collective-permute-start(bf16[1,1,768,128]{3,2,1,0:T(8,128)(2,1)} %param.11), channel_id=1, source_target_pairs={{0,8},{8,16},{16,24},{24,32},{32,40},{40,48},{48,56},{56,64},{64,7... | collective-permute-start | bytes 589832 | tf_op jit(solution)/shard_map/ppermute | solution.py:15
  4.2 27.2 %collective-permute-start.1 = (bf16[1,1,768,128]{3,2,1,0:T(8,128)(2,1)}, bf16[1,1,768,128]{3,2,1,0:T(8,128)(2,1)S(1)}, u32[]{:S(2)}, u32[]{:S(2)}) collective-permute-start(bf16[1,1,768,128]{3,2,1,0:T(8,128)(2,1)} %param.11), channel_id=1, source_target_pairs={{0,16},{8,24},{16,32},{24,40},{32,48},{40,56},{48,64},{56,72},{64,... | collective-permute-start | bytes 589832 | tf_op jit(solution)/shard_map/ppermute | solution.py:15
  9.5 27.9 %collective-permute-start.2 = (bf16[1,1,768,128]{2,3,1,0:T(8,128)(2,1)S(1)}, bf16[1,1,768,128]{2,3,1,0:T(8,128)(2,1)S(1)}, u32[]{:S(2)}, u32[]{:S(2)}) collective-permute-start(bf16[1,1,768,128]{2,3,1,0:T(8,128)(2,1)S(1)} %copy.17), channel_id=1, source_target_pairs={{0,8},{8,16},{16,24},{24,32},{32,40},{40,48},{48,56},{56,64},{64,7... | collective-permute-start | bytes 589832 | tf_op jit(solution)/shard_map/ppermute | solution.py:15
  13.9 25.3 %collective-permute-start.3 = (bf16[1,1,768,128]{2,3,1,0:T(8,128)(2,1)S(1)}, bf16[1,1,768,128]{2,3,1,0:T(8,128)(2,1)S(1)}, u32[]{:S(2)}, u32[]{:S(2)}) collective-permute-start(bf16[1,1,768,128]{2,3,1,0:T(8,128)(2,1)S(1)} %copy.17), channel_id=1, source_target_pairs={{0,16},{8,24},{16,32},{24,40},{32,48},{40,56},{48,64},{56,72},{64,... | collective-permute-start | bytes 589832 | tf_op jit(solution)/shard_map/ppermute | solution.py:15
  32.4 4.3 %copy-start.3 = (bf16[256,128]{1,0:T(8,128)(2,1)S(1)}, bf16[256,128]{1,0:T(8,128)(2,1)}, u32[]{:S(2)}) copy-start(bf16[256,128]{1,0:T(8,128)(2,1)} %param.10) | copy-start | bytes 196612
  39.1 1.8 %copy-start.1 = (bf16[1,1,768,128]{3,2,1,0:T(8,128)(2,1)S(1)}, bf16[1,1,768,128]{3,2,1,0:T(8,128)(2,1)}, u32[]{:S(2)}) copy-start(bf16[1,1,768,128]{3,2,1,0:T(8,128)(2,1)} %param.12) | copy-start | bytes 589828
  39.1 3.6 %slice-start = ((s8[8388608]{0:T(1024)(128)(4,1)}), s8[4194304]{0:T(1024)(128)(4,1)S(1)}, s32[]{:S(2)}) async-start(s8[8388608]{0:T(1024)(128)(4,1)} %bitcast.363), calls=%async_computation.1 | async-start | bytes 8388608
  40.9 2.3 %slice-start.1 = ((s8[8388608]{0:T(1024)(128)(4,1)}), s8[4194304]{0:T(1024)(128)(4,1)S(1)}, s32[]{:S(2)}) async-start(s8[8388608]{0:T(1024)(128)(4,1)} %bitcast.363), calls=%async_computation.2 | async-start | bytes 8388608
  78.2 14.1 %collective-permute-start.4 = (bf16[32,4096]{1,0:T(8,128)(2,1)S(1)}, bf16[32,4096]{1,0:T(8,128)(2,1)S(1)}, u32[]{:S(2)}, u32[]{:S(2)}) collective-permute-start(bf16[32,4096]{1,0:T(8,128)(2,1)S(1)} %reduce_sum.52), channel_id=1, source_target_pairs={{0,8},{8,16},{16,24},{24,32},{32,40},{40,48},{48,56},{56,64},{64,7... | collective-permute-start | bytes 786440 | tf_op jit(solution)/shard_map/ppermute | solution.py:32
where the time goes:
time: 93.5 us; the launch traced here: 93.1 us
  blocking collectives  32 us (34%)
  starting transfers between devices  17.5 us (19%)
  matrix products  12.8 us (14%)
  waiting for transfers between devices  11.8 us (13%)
  other arithmetic  9.91 us (11%)
  local copies, waits for them, and re-layouts  4.64 us (5%)
  between operations  4.34 us (5%)
    all_to_all x1, blocking collectives, sum_at_owner(): pieces = lax.all_to_all(in_blocks(value, dim, size), axis, 0, 0, tiled=True)  32 us
    ppermute x4, starting transfers between devices, shifted(): lax.ppermute(value, axis, [(source, source + steps) for source in range(f...  15.2 us
    ppermute x1, waiting for transfers between devices, shifted_2(): lax.ppermute(value, axis, [(i, (i + by) % size) for i in range(size)])  11.8 us
    reduce_sum x4, other arithmetic, partial_block(): row_total = jnp.sum(weights, axis=-1)  6.78 us
    dot_general x4, matrix products, partial_block(): jnp.einsum('rkgc,kch->rkgh', weights.astype(jnp.bfloat16), value_block, p...  5.91 us
    dot_general x4, matrix products, partial_block(): jnp.einsum('rkgh,kch->rkgc', query_heads, key_block, preferred_element_ty...  4.41 us
    dot_general x1, matrix products, on_device(): jnp.dot(attended, out_weight, preferred_element_type=jnp.float32)  2.52 us
    ppermute x1, starting transfers between devices, shifted_2(): lax.ppermute(value, axis, [(i, (i + by) % size) for i in range(size)])  2.31 us
  transfers between devices with their start and end apart: 5, of which 1 were waited for; matrix products, arithmetic and copies ran while one was open for 21% of the time, Pallas kernels for 0%

commit v1 on v0

v1 whole, which is shorter than its diff:
```python
import functools
import math

import jax
import jax.numpy as jnp
from jax import lax
from jax.experimental import pallas as pl
from jax.experimental.pallas import tpu as pltpu
from jax.sharding import PartitionSpec as P


HD = 128
GROUP = 8
MASKED = -1e30
LOG2E = 1.4426950408889634
BASE_FACTOR = LOG2E / math.sqrt(HD)
CHUNK = 256
ONES_ROWS = 16

VMEM = pl.BlockSpec(memory_space=pltpu.VMEM)
HBM = pl.BlockSpec(memory_space=pltpu.HBM)


def cache_facts(counts_ref, exps_ref, distance, width):
    index = lax.axis_index("section") - distance
    source = jnp.maximum(index, 0)
    live = jnp.full((1, width), jnp.where(index >= 0, counts_ref[source], 0), jnp.int32)
    key_exp = jnp.full((1, width), exps_ref[0, source], jnp.int32).astype(jnp.float32)
    value_exp = jnp.full((1, width), exps_ref[1, source], jnp.int32).astype(jnp.float32)
    return live, jnp.exp2(key_exp) * BASE_FACTOR, jnp.exp2(value_exp)


def facts_at(live_ref, scale_ref, distance):
    return (
        live_ref[distance : distance + 1, :],
        scale_ref[2 * distance : 2 * distance + 1, :],
        scale_ref[2 * distance + 1 : 2 * distance + 2, :],
    )


def fold_max(block):
    top = block[0:8]
    for at in range(8, block.shape[0], 8):
        top = jnp.maximum(top, block[at : at + 8])
    return top


def scores_of(key_block, q_ref, head):
    q = q_ref[:, head * HD : (head + 1) * HD]
    return lax.dot_general(key_block, q, (((1,), (1,)), ((), ())), preferred_element_type=jnp.float32)


def cache_scores(k_ref, q_ref, head, at, live):
    scores = scores_of(k_ref[at : at + CHUNK, :], q_ref, head)
    visible = lax.broadcasted_iota(jnp.int32, (CHUNK, HD), 0) < live[:, :HD] - at
    return jnp.concatenate(
        [jnp.where(visible, scores[:, n : n + HD], MASKED) for n in range(0, scores.shape[1], HD)], axis=1
    )


def fill_values(v_ref, vt_ref):
    vt_ref[:HD, :] = v_ref[...].T
    vt_ref[HD:, :] = jnp.ones((ONES_ROWS, vt_ref.shape[1]), jnp.bfloat16)


def own_kernel(
    counts_hbm, exps_hbm, q_hbm, nk_hbm, nv_hbm, k_hbm, v_hbm,
    acc_ref, peak_ref, total_ref, q_ref, live_ref, scale_ref,
    counts_ref, exps_ref, nk_ref, nv_ref, k_ref, v_ref,
    vt_ref, nvt_ref, s_ref, n_ref, p_ref, pn_ref, sems,
):
    pairs = (
        (counts_hbm, counts_ref), (exps_hbm, exps_ref), (q_hbm, q_ref), (nk_hbm, nk_ref),
        (k_hbm, k_ref), (nv_hbm, nv_ref), (v_hbm, v_ref),
    )
    copies = [pltpu.make_async_copy(source, target, sems.at[n]) for n, (source, target) in enumerate(pairs)]
    for copy in copies:
        copy.start()
    for copy in copies:
        copy.wait()
    rows = q_ref.shape[0]
    slots = k_ref.shape[0]
    facts = [cache_facts(counts_ref, exps_ref, distance, rows) for distance in range(3)]
    for distance, (live, factor, value_scale) in enumerate(facts):
        live_ref[distance : distance + 1, :] = live
        scale_ref[2 * distance : 2 * distance + 1, :] = factor
        scale_ref[2 * distance + 1 : 2 * distance + 2, :] = value_scale
    live, factor, value_scale = facts[0]
    fill_values(v_ref, vt_ref)
    fill_values(nv_ref, nvt_ref)

    def scores(head, slot):
        key = lax.broadcasted_iota(jnp.int32, (rows, rows), 0)
        row = lax.broadcasted_iota(jnp.int32, (rows, rows), 1)
        fresh = jnp.where(key <= row, scores_of(nk_ref[...], q_ref, head), MASKED)
        n_ref[slot] = fresh
        top = fold_max(fresh) * BASE_FACTOR
        for at in range(0, slots, CHUNK):
            cached = cache_scores(k_ref, q_ref, head, at, live)
            s_ref[slot, at : at + CHUNK, :] = cached
            top = jnp.maximum(top, fold_max(cached) * factor)
        return top

    top = scores(0, 0)
    for head in range(GROUP):
        slot = head % 2
        peak = jnp.max(top, axis=0, keepdims=True)
        if head + 1 < GROUP:
            top = scores(head + 1, 1 - slot)
        pn_ref[slot] = jnp.exp2(n_ref[slot] * BASE_FACTOR - peak).astype(jnp.bfloat16)
        for at in range(0, slots, CHUNK):
            p_ref[slot, at : at + CHUNK, :] = jnp.exp2(
                s_ref[slot, at : at + CHUNK, :] * factor - peak
            ).astype(jnp.bfloat16)
        fresh = jnp.dot(nvt_ref[...], pn_ref[slot], preferred_element_type=jnp.float32)
        cached = jnp.dot(vt_ref[...], p_ref[slot], preferred_element_type=jnp.float32)
        acc_ref[head * HD : (head + 1) * HD, :] = fresh[:HD] + value_scale * cached[:HD]
        total_ref[head : head + 1, :] = fresh[HD : HD + 1] + cached[HD : HD + 1]
        peak_ref[head : head + 1, :] = peak


def far_kernel(
    live_ref, scale_ref, q_ref, k_ref, v_ref, acc_in, peak_in, total_in,
    acc_ref, peak_ref, total_ref, vt_ref, s_ref, p_ref, *, distance,
):
    slots = k_ref.shape[0]
    live, factor, value_scale = facts_at(live_ref, scale_ref, distance)
    fill_values(v_ref, vt_ref)

    def scores(head, slot):
        top = None
        for at in range(0, slots, CHUNK):
            cached = cache_scores(k_ref, q_ref, head, at, live)
            s_ref[slot, at : at + CHUNK, :] = cached
            top = fold_max(cached) if top is None else jnp.maximum(top, fold_max(cached))
        return top

    top = scores(0, 0)
    for head in range(GROUP):
        slot = head % 2
        before = peak_in[head : head + 1, :]
        peak = jnp.maximum(before, jnp.max(top, axis=0, keepdims=True) * factor)
        kept = jnp.exp2(before - peak)
        if head + 1 < GROUP:
            top = scores(head + 1, 1 - slot)
        for at in range(0, slots, CHUNK):
            p_ref[slot, at : at + CHUNK, :] = jnp.exp2(
                s_ref[slot, at : at + CHUNK, :] * factor - peak
            ).astype(jnp.bfloat16)
        summed = jnp.dot(vt_ref[...], p_ref[slot], preferred_element_type=jnp.float32)
        at = slice(head * HD, (head + 1) * HD)
        acc_ref[at, :] = acc_in[at, :] * kept + value_scale * summed[:HD]
        total_ref[head : head + 1, :] = total_in[head : head + 1, :] * kept + summed[HD : HD + 1]
        peak_ref[head : head + 1, :] = peak


def last_weights_kernel(live_ref, scale_ref, q_ref, k_ref, peak_in, weights_ref, kept_ref, s_ref, *, distance):
    slots = k_ref.shape[0]
    live, factor, _ = facts_at(live_ref, scale_ref, distance)

    def scores(head, slot):
        top = None
        for at in range(0, slots, CHUNK):
            cached = cache_scores(k_ref, q_ref, head, at, live)
            s_ref[slot, at : at + CHUNK, :] = cached
            top = fold_max(cached) if top is None else jnp.maximum(top, fold_max(cached))
        return top

    top = scores(0, 0)
    for head in range(GROUP):
        slot = head % 2
        before = peak_in[head : head + 1, :]
        peak = jnp.maximum(before, jnp.max(top, axis=0, keepdims=True) * factor)
        kept_ref[head : head + 1, :] = jnp.exp2(before - peak)
        if head + 1 < GROUP:
            top = scores(head + 1, 1 - slot)
        for at in range(0, slots, CHUNK):
            weights_ref[head * slots + at : head * slots + at + CHUNK, :] = jnp.exp2(
                s_ref[slot, at : at + CHUNK, :] * factor - peak
            ).astype(jnp.bfloat16)


def row_plan(head_axis):
    index = lax.axis_index(head_axis)
    chip, core = index // 2, index % 2
    one, three = chip + 1 - 2 * (chip % 2), 3 - chip
    first = jnp.where(core == 0, one, three)
    second = jnp.where(core == 0, three, one)
    opposite = 3 - one
    return chip, core, first, second, opposite


def split_rows(turned_ref, send_ref, keep_ref):
    chip, core, first, second, opposite = row_plan("head")
    block = turned_ref.shape[0] // 8
    for out_ref, owner_core, chips in (
        (send_ref, 1 - core, (chip, first, second, opposite)),
        (keep_ref, core, (chip, second, first, opposite)),
    ):
        for at, owner in enumerate(chips):
            start = pl.multiple_of((2 * owner + owner_core) * block, block)
            out_ref[at * block : (at + 1) * block, :] = turned_ref[pl.ds(start, block), :]


def finish_kernel(
    scale_ref, weights_ref, v_ref, acc_ref, kept_ref, total_ref,
    send_ref, keep_ref, vt_ref, turned_ref, *, distance,
):
    slots = v_ref.shape[0]
    value_scale = scale_ref[2 * distance + 1 : 2 * distance + 2, :]
    fill_values(v_ref, vt_ref)
    for head in range(GROUP):
        summed = jnp.dot(
            vt_ref[...], weights_ref[head * slots : (head + 1) * slots, :],
            preferred_element_type=jnp.float32,
        )
        at = slice(head * HD, (head + 1) * HD)
        kept = kept_ref[head : head + 1, :]
        total = total_ref[head : head + 1, :] * kept + summed[HD : HD + 1]
        attended = (acc_ref[at, :] * kept + value_scale * summed[:HD]) / total
        turned_ref[:, at] = attended.T.astype(jnp.bfloat16)
    split_rows(turned_ref, send_ref, keep_ref)


def project_kernel(keep_ref, got_ref, w_ref, other_w_ref, send_out, keep_out, *, start):
    half, width = keep_out.shape
    step = 512
    for at in range(0, width, step):
        columns = slice(start + at, start + at + step)
        partial = jnp.dot(keep_ref[...], w_ref[:, columns], preferred_element_type=jnp.float32)
        partial += jnp.dot(got_ref[...], other_w_ref[:, columns], preferred_element_type=jnp.float32)
        keep_out[:, at : at + step] = partial[:half]
        send_out[:, at : at + step] = partial[half:].astype(jnp.bfloat16)


def params(mib):
    return pltpu.CompilerParams(vmem_limit_bytes=mib << 20)


def cost(keys, rows, products):
    wide = GROUP * rows * keys
    return pl.CostEstimate(flops=2 * products * wide * HD, transcendentals=wide, bytes_accessed=1 << 20)


def shifted(value, axis, steps):
    count = lax.axis_size(axis)
    return lax.ppermute(value, axis, [(i, i + steps) for i in range(count - steps)])


def core_pairs():
    return [(i, i ^ 1) for i in range(8)]


def chip_pairs(first):
    pairs = []
    for i in range(8):
        chip, core = i // 2, i % 2
        other = chip ^ 1 if (core == 0) == first else chip ^ 3
        pairs.append((i, 2 * other + core))
    return pairs


def on_device(
    queries, new_keys, new_values, cache_keys, cache_values, key_counts, scale_exps, out_weight
):
    rows = queries.shape[0]
    own_keys = cache_keys[0, 0]
    own_values = cache_values[0, 0]
    slots = own_keys.shape[0]
    exps = scale_exps.T
    wide = GROUP * HD
    f32, bf16 = jnp.float32, jnp.bfloat16

    keys_1 = shifted(own_keys, "section", 1)
    values_1 = shifted(own_values, "section", 1)
    other_weight = lax.ppermute(out_weight, "head", core_pairs())
    keys_2 = shifted(keys_1, "section", 1)
    values_2 = shifted(values_1, "section", 1)

    acc_shape = jax.ShapeDtypeStruct((wide, rows), f32)
    row_shape = jax.ShapeDtypeStruct((GROUP, rows), f32)
    vt = lambda n: pltpu.VMEM((HD + ONES_ROWS, n), bf16)
    pair = lambda n, t: pltpu.VMEM((2, n, rows), t)
    acc, peak, total, q, live, scale = pl.pallas_call(
        own_kernel,
        out_shape=(
            acc_shape, row_shape, row_shape, jax.ShapeDtypeStruct(queries.shape, bf16),
            jax.ShapeDtypeStruct((GROUP, rows), jnp.int32), row_shape,
        ),
        in_specs=[HBM] * 7,
        out_specs=(VMEM,) * 6,
        scratch_shapes=[
            pltpu.SMEM(key_counts.shape, jnp.int32), pltpu.SMEM(exps.shape, jnp.int32),
            pltpu.VMEM(new_keys.shape, bf16), pltpu.VMEM(new_values.shape, bf16),
            pltpu.VMEM(own_keys.shape, bf16), pltpu.VMEM(own_values.shape, bf16),
            vt(slots), vt(rows), pair(slots, f32), pair(rows, f32), pair(slots, bf16), pair(rows, bf16),
            pltpu.SemaphoreType.DMA((7,)),
        ],
        compiler_params=params(20),
        cost_estimate=cost(slots + rows, rows, 2),
        name="own",
    )(
        *(
            pltpu.with_memory_space_constraint(value, pltpu.HBM)
            for value in (key_counts, exps, queries, new_keys, new_values, own_keys, own_values)
        )
    )
    acc, peak, total = pl.pallas_call(
        functools.partial(far_kernel, distance=1),
        out_shape=(acc_shape, row_shape, row_shape),
        in_specs=[VMEM] * 8,
        out_specs=(VMEM, VMEM, VMEM),
        scratch_shapes=[vt(slots), pair(slots, f32), pair(slots, bf16)],
        compiler_params=params(16),
        cost_estimate=cost(slots, rows, 2),
        name="far",
    )(live, scale, q, keys_1, values_1, acc, peak, total)
    weights, kept = pl.pallas_call(
        functools.partial(last_weights_kernel, distance=2),
        out_shape=(jax.ShapeDtypeStruct((GROUP * slots, rows), bf16), row_shape),
        in_specs=[VMEM] * 5,
        out_specs=(VMEM, VMEM),
        scratch_shapes=[pair(slots, f32)],
        compiler_params=params(16),
        cost_estimate=cost(slots, rows, 1),
        name="last",
    )(live, scale, q, keys_2, peak)

    half, quarter, eighth = rows // 2, rows // 4, rows // 8
    send, keep = pl.pallas_call(
        functools.partial(finish_kernel, distance=2),
        out_shape=(jax.ShapeDtypeStruct((half, wide), bf16),) * 2,
        in_specs=[VMEM] * 6,
        out_specs=(VMEM, VMEM),
        scratch_shapes=[vt(slots), pltpu.VMEM((rows, wide), bf16)],
        compiler_params=params(16),
        cost_estimate=cost(slots, rows, 1),
        name="finish",
    )(scale, weights, values_2, acc, kept, total)
    got = lax.ppermute(send, "head", core_pairs())

    part = out_weight.shape[1] // 2
    size = lax.axis_size("section")
    pieces = []
    for start in (0, part):
        send, kept_rows = pl.pallas_call(
            functools.partial(project_kernel, start=start),
            out_shape=(jax.ShapeDtypeStruct((quarter, part), bf16), jax.ShapeDtypeStruct((quarter, part), f32)),
            in_specs=[VMEM] * 4,
            out_specs=(VMEM, VMEM),
            compiler_params=params(16),
            cost_estimate=pl.CostEstimate(
                flops=2 * rows * wide * part, transcendentals=0, bytes_accessed=1 << 20
            ),
            name="project",
        )(keep, got, out_weight, other_weight)
        first = lax.ppermute(send, "head", chip_pairs(True))
        two = kept_rows + first.astype(f32)
        second = lax.ppermute(two[eighth:].astype(bf16), "head", chip_pairs(False))
        done = (two[:eighth] + second.astype(f32)).astype(bf16)
        pieces.append(lax.ppermute(done, "section", [(i, (i + 1) % size) for i in range(size)]))
    return jnp.concatenate(pieces, axis=1).astype(f32)


def solution(mesh):
    in_specs = (
        P("section", "head"),
        P("section", "head"),
        P("section", "head"),
        P("section", "head", None, None),
        P("section", "head", None, None),
        P(),
        P(),
        P("head", None),
    )
    out_specs = P(("section", "head"), None)
    return jax.shard_map(on_device, mesh=mesh, in_specs=in_specs, out_specs=out_specs, check_vma=False)
```

time: 93.5 us -> 74.4 us (0.80)
  blocking collectives: 32 us -> 0 us
  starting transfers between devices: 17.5 us -> 40.8 us
  matrix products: 12.8 us -> 0 us
  Pallas kernels: 0 us -> 12.6 us
  other arithmetic: 9.91 us -> 0.99 us
  waiting for transfers between devices: 11.8 us -> 19.3 us
  local copies, waits for them, and re-layouts: 4.64 us -> 0.04 us
  between operations: 4.34 us -> 0.19 us
    all_to_all x1 -> x0, blocking collectives: 32 us -> none  [sum_at_owner(): pieces = lax.all_to_all(in_blocks(value, dim, size), axis, 0, 0, tiled=True)]
    ppermute x5 -> x12, starting transfers between devices: 17.5 us -> 40.8 us  [the longest x1 12.6 us: on_device(): other_weight = lax.ppermute(out_weight, 'head', core_pairs())]
    dot_general x9 -> x0, matrix products: 12.8 us -> none  [the longest x4 5.91 us: partial_block(): jnp.einsum('rkgc,kch->rkgh', weights.astype(jnp.bfloat16), value_block, p...]
    pallas_call x0 -> x6, Pallas kernels: none -> 12.6 us  [the longest x1 4.47 us: on_device(): pl.pallas_call(own_kernel, out_shape=(acc_shape, row_shape, row_shape, ja...]
    ppermute x5 -> x12, waiting for transfers between devices: 11.8 us -> 19.3 us  [the longest x2 11.4 us: on_device(): lax.ppermute(done, 'section', [(i, (i + 1) % size) for i in range(size)])]
    reduce_sum x5 -> x0, other arithmetic: 7.12 us -> none  [the longest x4 6.78 us: partial_block(): row_total = jnp.sum(weights, axis=-1)]
    dynamic_slice x2 -> x0, local copies, waits for them, and re-layouts: 3.03 us -> none  [the longest x1 1.58 us: cache_terms(): value_scale = jnp.exp2(scale_exps[source, 1].astype(jnp.float32))]
    and x3 -> x0, other arithmetic: 1.9 us -> none  [cache_terms(): visible = ((slots < key_counts[source]) & (index >= 0))[None, None, None, :]]
  transfers between devices with their start and end apart: 5 -> 12, of which waited for: 1 -> 9; matrix products, arithmetic and copies ran while one was open for 21% -> 0% of each run, Pallas kernels for 0% -> 15%
where the time goes in v1:
time: 74.4 us; the launch traced here: 73.9 us
  starting transfers between devices  40.8 us (55%)
  waiting for transfers between devices  19.3 us (26%)
  Pallas kernels  12.6 us (17%)
  other arithmetic  0.99 us (1%)
    ppermute x1, starting transfers between devices, on_device(): other_weight = lax.ppermute(out_weight, 'head', core_pairs())  12.6 us
    ppermute x2, waiting for transfers between devices, on_device(): lax.ppermute(done, 'section', [(i, (i + 1) % size) for i in range(size)])  11.4 us
    ppermute x4, starting transfers between devices, shifted(): lax.ppermute(value, axis, [(i, i + steps) for i in range(count - steps)])  10.6 us
    ppermute x2, starting transfers between devices, on_device(): first = lax.ppermute(send, 'head', chip_pairs(True))  6.49 us
    pallas_call x1, Pallas kernels, on_device(): pl.pallas_call(own_kernel, out_shape=(acc_shape, row_shape, row_shape, ja...  4.47 us
    ppermute x2, starting transfers between devices, on_device(): second = lax.ppermute(two[eighth:].astype(bf16), 'head', chip_pairs(False))  4.09 us
    ppermute x2, starting transfers between devices, on_device(): lax.ppermute(done, 'section', [(i, (i + 1) % size) for i in range(size)])  3.84 us
    ppermute x4, waiting for transfers between devices, shifted(): lax.ppermute(value, axis, [(i, i + steps) for i in range(count - steps)])  3.45 us
  transfers between devices with their start and end apart: 12, of which 9 were waited for; matrix products, arithmetic and copies ran while one was open for 0% of the time, Pallas kernels for 15%

profile of v1, /device:TPU:1, one launch (start us, length us, event | category | flops | bytes accessed | tf_op | source)
XLA Modules:
  0.0 73.9 jit_solution(7193747899292526341)
XLA Ops:
  0.0 0.0 copy-start
  0.0 12.6 %collective-permute-start.5 = (bf16[1024,4096]{1,0:T(8,128)(2,1)}, bf16[1024,4096]{1,0:T(8,128)(2,1)S(1)}, u32[]{:S(2)}, u32[]{:S(2)}) collective-permute-start(bf16[1024,4096]{1,0:T(8,128)(2,1)} %w_ref.3), channel_id=1, source_target_pairs={{0,1},{1,0},{2,3},{3,2},{4,5},{5,4},{6,7},{7,6},{8,9},{9,8},{10,11... | collective-permute-start | bytes 25165832 | tf_op jit(solution)/shard_map/ppermute | solution.py:276
  12.6 1.3 %collective-permute-start = (bf16[768,128]{1,0:T(8,128)(2,1)}, bf16[768,128]{1,0:T(8,128)(2,1)S(1)}, u32[]{:S(2)}, u32[]{:S(2)}) collective-permute-start(bf16[768,128]{1,0:T(8,128)(2,1)} %bitcast.3), channel_id=1, source_target_pairs={{0,8},{8,16},{16,24},{24,32},{32,40},{40,48},{48,56},{56,64},{64,7... | collective-permute-start | bytes 589832 | tf_op jit(solution)/shard_map/ppermute | solution.py:247
  14.0 1.3 %collective-permute-start.2 = (bf16[768,128]{1,0:T(8,128)(2,1)}, bf16[768,128]{1,0:T(8,128)(2,1)S(1)}, u32[]{:S(2)}, u32[]{:S(2)}) collective-permute-start(bf16[768,128]{1,0:T(8,128)(2,1)} %bitcast.5), channel_id=1, source_target_pairs={{0,8},{8,16},{16,24},{24,32},{32,40},{40,48},{48,56},{56,64},{64,7... | collective-permute-start | bytes 589832 | tf_op jit(solution)/shard_map/ppermute | solution.py:247
  15.3 3.2 %collective-permute-done.k_ref = bf16[768,128]{1,0:T(8,128)(2,1)S(1)} collective-permute-done((bf16[768,128]{1,0:T(8,128)(2,1)}, bf16[768,128]{1,0:T(8,128)(2,1)S(1)}, u32[]{:S(2)}, u32[]{:S(2)}) %collective-permute-start) | collective-permute-done | bytes 196640 | tf_op jit(solution)/shard_map/ppermute | solution.py:247
  18.5 4.0 %collective-permute-start.1 = (bf16[768,128]{1,0:T(8,128)(2,1)S(1)}, bf16[768,128]{1,0:T(8,128)(2,1)S(1)}, u32[]{:S(2)}, u32[]{:S(2)}) collective-permute-start(bf16[768,128]{1,0:T(8,128)(2,1)S(1)} %collective-permute-done.k_ref), channel_id=1, source_target_pairs={{0,8},{8,16},{16,24},{24,32},{32,40},{40,48},{48,56},{56,64},{64,7... | collective-permute-start | bytes 589832 | tf_op jit(solution)/shard_map/ppermute | solution.py:247
  22.5 0.2 collective-permute-done.2.v_ref
  22.7 4.0 %collective-permute-start.3 = (bf16[768,128]{1,0:T(8,128)(2,1)S(1)}, bf16[768,128]{1,0:T(8,128)(2,1)S(1)}, u32[]{:S(2)}, u32[]{:S(2)}) collective-permute-start(bf16[768,128]{1,0:T(8,128)(2,1)S(1)} %collective-permute-done.2.v_ref), channel_id=1, source_target_pairs={{0,8},{8,16},{16,24},{24,32},{32,40},{40,48},{48,56},{56,64},{64,7... | collective-permute-start | bytes 589832 | tf_op jit(solution)/shard_map/ppermute | solution.py:247
  26.7 4.5 %own.1 = (f32[1024,256]{1,0:T(8,128)S(1)}, f32[8,256]{1,0:T(8,128)S(1)}, f32[8,256]{1,0:T(8,128)S(1)}, bf16[256,1024]{1,0:T(8,128)(2,1)S(1)}, s32[8,256]{1,0:T(8,128)S(1)}, /*index=5*/f32[8,256]{1,0:T(8,128)S(1)}) custom-call(s32[96]{0:T(128)} %counts_hbm.1, s32[2,96]{1,0:T(2,128)} %bitcast.7, bf16[256,1024]{1,0:T(8,128)(2,1)} %q_hbm.1, ...), custom_call_target="tpu_custom_call" | custom-call | flops 1073741824 | bytes 1048576 | tf_op jit(solution)/shard_map/own/pallas_call | solution.py:284
  31.2 2.7 %far.1 = (f32[1024,256]{1,0:T(8,128)S(1)}, f32[8,256]{1,0:T(8,128)S(1)}, f32[8,256]{1,0:T(8,128)S(1)}) custom-call(s32[8,256]{1,0:T(8,128)S(1)} %get-tuple-element.23.live_ref, f32[8,256]{1,0:T(8,128)S(1)} %get-tuple-element.22.scale_ref, bf16[256,1024]{1,0:T(8,128)(2,1)S(1)} %get-tuple-element.24.q_ref, bf16[768,128]{1,0:T(8,128)(2,1)S(1)} %collective-permute-done.k_ref, ...), custom_call_target="tpu_custom_call" | custom-call | flops 805306368 | bytes 1048576 | tf_op jit(solution)/shard_map/far/pallas_call | solution.py:308
  33.9 0.0 collective-permute-done.1.k_ref
  33.9 2.0 %last.1 = (bf16[6144,256]{1,0:T(8,128)(2,1)S(1)}, f32[8,256]{1,0:T(8,128)S(1)}) custom-call(s32[8,256]{1,0:T(8,128)S(1)} %get-tuple-element.23.live_ref, f32[8,256]{1,0:T(8,128)S(1)} %get-tuple-element.22.scale_ref, bf16[256,1024]{1,0:T(8,128)(2,1)S(1)} %get-tuple-element.24.q_ref, bf16[768,128]{1,0:T(8,128)(2,1)S(1)} %collective-permute-done.1.k_ref, ...), custom_call_target="tpu_custom_call" | custom-call | flops 402653184 | bytes 1048576 | tf_op jit(solution)/shard_map/last/pallas_call | solution.py:318
  35.9 0.0 collective-permute-done.3.v_ref
  35.9 0.9 %finish.1 = (bf16[128,1024]{1,0:T(8,128)(2,1)S(1)}, bf16[128,1024]{1,0:T(8,128)(2,1)S(1)}) custom-call(f32[8,256]{1,0:T(8,128)S(1)} %get-tuple-element.22.scale_ref, bf16[6144,256]{1,0:T(8,128)(2,1)S(1)} %get-tuple-element.29.weights_ref, bf16[768,128]{1,0:T(8,128)(2,1)S(1)} %collective-permute-done.3.v_ref, f32[1024,256]{1,0:T(8,128)S(1)} %get-tuple-element.30.acc_ref, ...), custom_call_target="tpu_custom_call" | custom-call | flops 402653184 | bytes 1048576 | tf_op jit(solution)/shard_map/finish/pallas_call | solution.py:330
  36.8 3.1 %collective-permute-start.4 = (bf16[128,1024]{1,0:T(8,128)(2,1)S(1)}, bf16[128,1024]{1,0:T(8,128)(2,1)S(1)}, u32[]{:S(2)}, u32[]{:S(2)}) collective-permute-start(bf16[128,1024]{1,0:T(8,128)(2,1)S(1)} %get-tuple-element.34), channel_id=1, source_target_pairs={{0,1},{1,0},{2,3},{3,2},{4,5},{5,4},{6,7},{7,6},{8,9},{9,8},{10,11... | collective-permute-start | bytes 786440 | tf_op jit(solution)/shard_map/ppermute | solution.py:340
  39.9 1.1 %collective-permute-done.4.got_ref = bf16[128,1024]{1,0:T(8,128)(2,1)S(1)} collective-permute-done((bf16[128,1024]{1,0:T(8,128)(2,1)S(1)}, bf16[128,1024]{1,0:T(8,128)(2,1)S(1)}, u32[]{:S(2)}, u32[]{:S(2)}) %collective-permute-start.4) | collective-permute-done | bytes 262176 | tf_op jit(solution)/shard_map/ppermute | solution.py:340
  41.1 0.0 collective-permute-done.5.other_w_ref
  41.1 0.0 copy-done
  41.1 1.3 %project.2 = (bf16[64,2048]{1,0:T(8,128)(2,1)S(1)}, f32[64,2048]{1,0:T(8,128)S(1)}) custom-call(bf16[128,1024]{1,0:T(8,128)(2,1)S(1)} %get-tuple-element.33.keep_ref, bf16[128,1024]{1,0:T(8,128)(2,1)S(1)} %collective-permute-done.4.got_ref, bf16[1024,4096]{1,0:T(8,128)(2,1)S(1)} %copy-done, bf16[1024,4096]{1,0:T(8,128)(2,1)S(1)} %collective-permute-done.5.other_w_ref), custom_call_target="tpu_custom_call" | custom-call | flops 1073741824 | bytes 1048576 | tf_op jit(solution)/shard_map/project/pallas_call | solution.py:346
  42.4 1.9 %collective-permute-start.6 = (bf16[64,2048]{1,0:T(8,128)(2,1)S(1)}, bf16[64,2048]{1,0:T(8,128)(2,1)S(1)}, u32[]{:S(2)}, u32[]{:S(2)}) collective-permute-start(bf16[64,2048]{1,0:T(8,128)(2,1)S(1)} %get-tuple-element.36), channel_id=1, source_target_pairs={{0,2},{1,7},{2,0},{3,5},{4,6},{5,3},{6,4},{7,1},{8,10},{9,15},{10,... | collective-permute-start | bytes 786440 | tf_op jit(solution)/shard_map/ppermute | solution.py:357
  44.3 1.3 %project.3 = (bf16[64,2048]{1,0:T(8,128)(2,1)S(1)}, f32[64,2048]{1,0:T(8,128)S(1)}) custom-call(bf16[128,1024]{1,0:T(8,128)(2,1)S(1)} %get-tuple-element.33.keep_ref, bf16[128,1024]{1,0:T(8,128)(2,1)S(1)} %collective-permute-done.4.got_ref, bf16[1024,4096]{1,0:T(8,128)(2,1)S(1)} %copy-done, bf16[1024,4096]{1,0:T(8,128)(2,1)S(1)} %collective-permute-done.5.other_w_ref), custom_call_target="tpu_custom_call" | custom-call | flops 1073741824 | bytes 1048576 | tf_op jit(solution)/shard_map/project/pallas_call | solution.py:346
  45.6 4.6 %collective-permute-start.9 = (bf16[64,2048]{1,0:T(8,128)(2,1)S(1)}, bf16[64,2048]{1,0:T(8,128)(2,1)S(1)}, u32[]{:S(2)}, u32[]{:S(2)}) collective-permute-start(bf16[64,2048]{1,0:T(8,128)(2,1)S(1)} %get-tuple-element.38), channel_id=1, source_target_pairs={{0,2},{1,7},{2,0},{3,5},{4,6},{5,3},{6,4},{7,1},{8,10},{9,15},{10,... | collective-permute-start | bytes 786440 | tf_op jit(solution)/shard_map/ppermute | solution.py:357
  50.2 0.5 collective-permute-done.6
  50.8 1.9 %collective-permute-start.7 = (bf16[32,2048]{1,0:T(8,128)(2,1)S(1)}, bf16[32,2048]{1,0:T(8,128)(2,1)S(1)}, u32[]{:S(2)}, u32[]{:S(2)}) collective-permute-start(bf16[32,2048]{1,0:T(8,128)(2,1)S(1)} %slice.31), channel_id=1, source_target_pairs={{0,6},{1,3},{2,4},{3,1},{4,2},{5,7},{6,0},{7,5},{8,14},{9,11},{10,... | collective-permute-start | bytes 393224 | tf_op jit(solution)/shard_map/ppermute | solution.py:359
  52.7 1.2 %collective-permute-done.9 = bf16[64,2048]{1,0:T(8,128)(2,1)S(1)} collective-permute-done((bf16[64,2048]{1,0:T(8,128)(2,1)S(1)}, bf16[64,2048]{1,0:T(8,128)(2,1)S(1)}, u32[]{:S(2)}, u32[]{:S(2)}) %collective-permute-start.9) | collective-permute-done | bytes 262176 | tf_op jit(solution)/shard_map/ppermute | solution.py:357
  53.9 0.1 convert_add_fusion
  54.0 2.2 %collective-permute-start.10 = (bf16[32,2048]{1,0:T(8,128)(2,1)S(1)}, bf16[32,2048]{1,0:T(8,128)(2,1)S(1)}, u32[]{:S(2)}, u32[]{:S(2)}) collective-permute-start(bf16[32,2048]{1,0:T(8,128)(2,1)S(1)} %slice.30), channel_id=1, source_target_pairs={{0,6},{1,3},{2,4},{3,1},{4,2},{5,7},{6,0},{7,5},{8,14},{9,11},{10,... | collective-permute-start | bytes 393224 | tf_op jit(solution)/shard_map/ppermute | solution.py:359
  56.2 0.3 collective-permute-done.7
  56.5 1.9 %collective-permute-start.8 = (bf16[32,2048]{1,0:T(8,128)(2,1)S(1)}, bf16[32,2048]{1,0:T(8,128)(2,1)S(1)}, u32[]{:S(2)}, u32[]{:S(2)}) collective-permute-start(bf16[32,2048]{1,0:T(8,128)(2,1)S(1)} %fusion.1), channel_id=1, source_target_pairs={{0,8},{8,16},{16,24},{24,32},{32,40},{40,48},{48,56},{56,64},{64,7... | collective-permute-start | bytes 393224 | tf_op jit(solution)/shard_map/ppermute | solution.py:361
  58.4 1.3 %collective-permute-done.10 = bf16[32,2048]{1,0:T(8,128)(2,1)S(1)} collective-permute-done((bf16[32,2048]{1,0:T(8,128)(2,1)S(1)}, bf16[32,2048]{1,0:T(8,128)(2,1)S(1)}, u32[]{:S(2)}, u32[]{:S(2)}) %collective-permute-start.10) | collective-permute-done | bytes 131104 | tf_op jit(solution)/shard_map/ppermute | solution.py:359
  59.7 1.9 %collective-permute-start.11 = (bf16[32,2048]{1,0:T(8,128)(2,1)S(1)}, bf16[32,2048]{1,0:T(8,128)(2,1)S(1)}, u32[]{:S(2)}, u32[]{:S(2)}) collective-permute-start(bf16[32,2048]{1,0:T(8,128)(2,1)S(1)} %fusion), channel_id=1, source_target_pairs={{0,8},{8,16},{16,24},{24,32},{32,40},{40,48},{48,56},{56,64},{64,7... | collective-permute-start | bytes 393224 | tf_op jit(solution)/shard_map/ppermute | solution.py:361
  61.7 7.4 %collective-permute-done.8 = bf16[32,2048]{1,0:T(8,128)(2,1)S(1)} collective-permute-done((bf16[32,2048]{1,0:T(8,128)(2,1)S(1)}, bf16[32,2048]{1,0:T(8,128)(2,1)S(1)}, u32[]{:S(2)}, u32[]{:S(2)}) %collective-permute-start.8) | collective-permute-done | bytes 131104 | tf_op jit(solution)/shard_map/ppermute | solution.py:361
  69.0 4.1 %collective-permute-done.11 = bf16[32,2048]{1,0:T(8,128)(2,1)S(1)} collective-permute-done((bf16[32,2048]{1,0:T(8,128)(2,1)S(1)}, bf16[32,2048]{1,0:T(8,128)(2,1)S(1)}, u32[]{:S(2)}, u32[]{:S(2)}) %collective-permute-start.11) | collective-permute-done | bytes 131104 | tf_op jit(solution)/shard_map/ppermute | solution.py:361
  73.1 0.8 %maximum_convert_fusion = f32[32,4096]{1,0:T(8,128)} fusion(bf16[32,2048]{1,0:T(8,128)(2,1)S(1)} %collective-permute-done.11, bf16[32,2048]{1,0:T(8,128)(2,1)S(1)} %collective-permute-done.8), kind=kLoop, calls=%fused_computation.8 | loop fusion | flops 524288 | bytes 786432 | tf_op jit(solution)/shard_map/convert_element_type | solution.py:362
  (5 shorter events, 0.1 us)
Async XLA Ops:
  0.0 41.1 %copy-start = (bf16[1024,4096]{1,0:T(8,128)(2,1)S(1)}, bf16[1024,4096]{1,0:T(8,128)(2,1)}, u32[]{:S(2)}) copy-start(bf16[1024,4096]{1,0:T(8,128)(2,1)} %w_ref.3) | copy-start | bytes 25165828
  0.0 41.1 %collective-permute-start.5 = (bf16[1024,4096]{1,0:T(8,128)(2,1)}, bf16[1024,4096]{1,0:T(8,128)(2,1)S(1)}, u32[]{:S(2)}, u32[]{:S(2)}) collective-permute-start(bf16[1024,4096]{1,0:T(8,128)(2,1)} %w_ref.3), channel_id=1, source_target_pairs={{0,1},{1,0},{2,3},{3,2},{4,5},{5,4},{6,7},{7,6},{8,9},{9,8},{10,11... | collective-permute-start | bytes 25165832 | tf_op jit(solution)/shard_map/ppermute | solution.py:276
  12.6 5.9 %collective-permute-start = (bf16[768,128]{1,0:T(8,128)(2,1)}, bf16[768,128]{1,0:T(8,128)(2,1)S(1)}, u32[]{:S(2)}, u32[]{:S(2)}) collective-permute-start(bf16[768,128]{1,0:T(8,128)(2,1)} %bitcast.3), channel_id=1, source_target_pairs={{0,8},{8,16},{16,24},{24,32},{32,40},{40,48},{48,56},{56,64},{64,7... | collective-permute-start | bytes 589832 | tf_op jit(solution)/shard_map/ppermute | solution.py:247
  14.0 8.8 %collective-permute-start.2 = (bf16[768,128]{1,0:T(8,128)(2,1)}, bf16[768,128]{1,0:T(8,128)(2,1)S(1)}, u32[]{:S(2)}, u32[]{:S(2)}) collective-permute-start(bf16[768,128]{1,0:T(8,128)(2,1)} %bitcast.5), channel_id=1, source_target_pairs={{0,8},{8,16},{16,24},{24,32},{32,40},{40,48},{48,56},{56,64},{64,7... | collective-permute-start | bytes 589832 | tf_op jit(solution)/shard_map/ppermute | solution.py:247
  18.5 15.4 %collective-permute-start.1 = (bf16[768,128]{1,0:T(8,128)(2,1)S(1)}, bf16[768,128]{1,0:T(8,128)(2,1)S(1)}, u32[]{:S(2)}, u32[]{:S(2)}) collective-permute-start(bf16[768,128]{1,0:T(8,128)(2,1)S(1)} %collective-permute-done.k_ref), channel_id=1, source_target_pairs={{0,8},{8,16},{16,24},{24,32},{32,40},{40,48},{48,56},{56,64},{64,7... | collective-permute-start | bytes 589832 | tf_op jit(solution)/shard_map/ppermute | solution.py:247
  22.7 13.2 %collective-permute-start.3 = (bf16[768,128]{1,0:T(8,128)(2,1)S(1)}, bf16[768,128]{1,0:T(8,128)(2,1)S(1)}, u32[]{:S(2)}, u32[]{:S(2)}) collective-permute-start(bf16[768,128]{1,0:T(8,128)(2,1)S(1)} %collective-permute-done.2.v_ref), channel_id=1, source_target_pairs={{0,8},{8,16},{16,24},{24,32},{32,40},{40,48},{48,56},{56,64},{64,7... | collective-permute-start | bytes 589832 | tf_op jit(solution)/shard_map/ppermute | solution.py:247
  36.8 4.3 %collective-permute-start.4 = (bf16[128,1024]{1,0:T(8,128)(2,1)S(1)}, bf16[128,1024]{1,0:T(8,128)(2,1)S(1)}, u32[]{:S(2)}, u32[]{:S(2)}) collective-permute-start(bf16[128,1024]{1,0:T(8,128)(2,1)S(1)} %get-tuple-element.34), channel_id=1, source_target_pairs={{0,1},{1,0},{2,3},{3,2},{4,5},{5,4},{6,7},{7,6},{8,9},{9,8},{10,11... | collective-permute-start | bytes 786440 | tf_op jit(solution)/shard_map/ppermute | solution.py:340
  42.4 8.3 %collective-permute-start.6 = (bf16[64,2048]{1,0:T(8,128)(2,1)S(1)}, bf16[64,2048]{1,0:T(8,128)(2,1)S(1)}, u32[]{:S(2)}, u32[]{:S(2)}) collective-permute-start(bf16[64,2048]{1,0:T(8,128)(2,1)S(1)} %get-tuple-element.36), channel_id=1, source_target_pairs={{0,2},{1,7},{2,0},{3,5},{4,6},{5,3},{6,4},{7,1},{8,10},{9,15},{10,... | collective-permute-start | bytes 786440 | tf_op jit(solution)/shard_map/ppermute | solution.py:357
  45.6 8.3 %collective-permute-start.9 = (bf16[64,2048]{1,0:T(8,128)(2,1)S(1)}, bf16[64,2048]{1,0:T(8,128)(2,1)S(1)}, u32[]{:S(2)}, u32[]{:S(2)}) collective-permute-start(bf16[64,2048]{1,0:T(8,128)(2,1)S(1)} %get-tuple-element.38), channel_id=1, source_target_pairs={{0,2},{1,7},{2,0},{3,5},{4,6},{5,3},{6,4},{7,1},{8,10},{9,15},{10,... | collective-permute-start | bytes 786440 | tf_op jit(solution)/shard_map/ppermute | solution.py:357
  50.8 5.7 %collective-permute-start.7 = (bf16[32,2048]{1,0:T(8,128)(2,1)S(1)}, bf16[32,2048]{1,0:T(8,128)(2,1)S(1)}, u32[]{:S(2)}, u32[]{:S(2)}) collective-permute-start(bf16[32,2048]{1,0:T(8,128)(2,1)S(1)} %slice.31), channel_id=1, source_target_pairs={{0,6},{1,3},{2,4},{3,1},{4,2},{5,7},{6,0},{7,5},{8,14},{9,11},{10,... | collective-permute-start | bytes 393224 | tf_op jit(solution)/shard_map/ppermute | solution.py:359
  54.0 5.7 %collective-permute-start.10 = (bf16[32,2048]{1,0:T(8,128)(2,1)S(1)}, bf16[32,2048]{1,0:T(8,128)(2,1)S(1)}, u32[]{:S(2)}, u32[]{:S(2)}) collective-permute-start(bf16[32,2048]{1,0:T(8,128)(2,1)S(1)} %slice.30), channel_id=1, source_target_pairs={{0,6},{1,3},{2,4},{3,1},{4,2},{5,7},{6,0},{7,5},{8,14},{9,11},{10,... | collective-permute-start | bytes 393224 | tf_op jit(solution)/shard_map/ppermute | solution.py:359
  56.5 12.5 %collective-permute-start.8 = (bf16[32,2048]{1,0:T(8,128)(2,1)S(1)}, bf16[32,2048]{1,0:T(8,128)(2,1)S(1)}, u32[]{:S(2)}, u32[]{:S(2)}) collective-permute-start(bf16[32,2048]{1,0:T(8,128)(2,1)S(1)} %fusion.1), channel_id=1, source_target_pairs={{0,8},{8,16},{16,24},{24,32},{32,40},{40,48},{48,56},{56,64},{64,7... | collective-permute-start | bytes 393224 | tf_op jit(solution)/shard_map/ppermute | solution.py:361
  59.7 13.3 %collective-permute-start.11 = (bf16[32,2048]{1,0:T(8,128)(2,1)S(1)}, bf16[32,2048]{1,0:T(8,128)(2,1)S(1)}, u32[]{:S(2)}, u32[]{:S(2)}) collective-permute-start(bf16[32,2048]{1,0:T(8,128)(2,1)S(1)} %fusion), channel_id=1, source_target_pairs={{0,8},{8,16},{16,24},{24,32},{32,40},{40,48},{48,56},{56,64},{64,7... | collective-permute-start | bytes 393224 | tf_op jit(solution)/shard_map/ppermute | solution.py:361

commit v2 on v1

v2 whole, which is shorter than its diff:
```python
import functools
import math

import jax
import jax.numpy as jnp
from jax import lax
from jax.experimental import pallas as pl
from jax.experimental.pallas import tpu as pltpu
from jax.sharding import PartitionSpec as P


HD = 128
GROUP = 8
MASKED = -1e30
LOG2E = 1.4426950408889634
BASE_FACTOR = LOG2E / math.sqrt(HD)
CHUNK = 256
ONES_ROWS = 16

VMEM = pl.BlockSpec(memory_space=pltpu.VMEM)
HBM = pl.BlockSpec(memory_space=pltpu.HBM)


def cache_facts(counts_ref, exps_ref, distance, width):
    index = lax.axis_index("section") - distance
    source = jnp.maximum(index, 0)
    live = jnp.full((1, width), jnp.where(index >= 0, counts_ref[source], 0), jnp.int32)
    key_exp = jnp.full((1, width), exps_ref[0, source], jnp.int32).astype(jnp.float32)
    value_exp = jnp.full((1, width), exps_ref[1, source], jnp.int32).astype(jnp.float32)
    factor = jnp.where(live > 0, jnp.exp2(key_exp), 1.0) * BASE_FACTOR
    return live, factor, jnp.exp2(value_exp)


def facts_at(live_ref, scale_ref, distance):
    return (
        live_ref[distance : distance + 1, :],
        scale_ref[2 * distance : 2 * distance + 1, :],
        scale_ref[2 * distance + 1 : 2 * distance + 2, :],
    )


def fold_max(block):
    top = block[0:8]
    for at in range(8, block.shape[0], 8):
        top = jnp.maximum(top, block[at : at + 8])
    return top


def scores_of(key_block, q_ref, head):
    q = q_ref[:, head * HD : (head + 1) * HD]
    return lax.dot_general(key_block, q, (((1,), (1,)), ((), ())), preferred_element_type=jnp.float32)


def cache_scores(keys_ref, q_ref, head, at):
    return scores_of(keys_ref[at : at + CHUNK, :], q_ref, head)


def fill_keys(k_ref, spare_ref, live, keys_ref):
    keys = k_ref[...].astype(jnp.float32)
    spare = jnp.where(live[:, :HD] > 0, keys[0:1], spare_ref[0:1, :].astype(jnp.float32))
    slot = lax.broadcasted_iota(jnp.int32, keys.shape, 0)
    keys_ref[...] = jnp.where(slot < live[:, :HD], keys, spare).astype(jnp.bfloat16)


def fill_values(v_ref, vt_ref, live=None):
    slots = v_ref.shape[0]
    values = v_ref[...]
    ones = jnp.ones((ONES_ROWS, slots), jnp.float32)
    if live is not None:
        slot = lax.broadcasted_iota(jnp.int32, values.shape, 0)
        values = jnp.where(slot < live[:, :HD], values.astype(jnp.float32), 0.0).astype(jnp.bfloat16)
        lane = lax.broadcasted_iota(jnp.int32, ones.shape, 1)
        ones = jnp.where(lane < jnp.concatenate([live[:, :HD]] * (slots // HD), axis=1), ones, 0.0)
    vt_ref[:HD, :] = values.T
    vt_ref[HD:, :] = ones.astype(jnp.bfloat16)


def near_kernel(
    counts_hbm, exps_hbm, q_hbm, nk_hbm, nv_hbm, k_hbm, v_hbm, far_k_ref, far_v_ref,
    acc_ref, peak_ref, total_ref, q_ref, live_ref, scale_ref, nk_ref,
    counts_ref, exps_ref, nv_ref, k_ref, v_ref, keys_ref, far_keys_ref,
    vt_ref, far_vt_ref, nvt_ref, s_ref, far_s_ref, n_ref, p_ref, far_p_ref, pn_ref, sems,
):
    pairs = (
        (q_hbm, q_ref), (counts_hbm, counts_ref), (exps_hbm, exps_ref), (nk_hbm, nk_ref),
        (k_hbm, k_ref), (nv_hbm, nv_ref), (v_hbm, v_ref),
    )
    copies = [pltpu.make_async_copy(source, target, sems.at[n]) for n, (source, target) in enumerate(pairs)]
    for copy in copies:
        copy.start()
    for copy in copies:
        copy.wait()
    rows = q_ref.shape[0]
    slots = k_ref.shape[0]
    facts = [cache_facts(counts_ref, exps_ref, distance, rows) for distance in range(3)]
    for distance, (live, factor, value_scale) in enumerate(facts):
        live_ref[distance : distance + 1, :] = live
        scale_ref[2 * distance : 2 * distance + 1, :] = factor
        scale_ref[2 * distance + 1 : 2 * distance + 2, :] = value_scale
    fill_keys(k_ref, nk_ref, facts[0][0], keys_ref)
    fill_keys(far_k_ref, nk_ref, facts[1][0], far_keys_ref)
    fill_values(nv_ref, nvt_ref)
    fill_values(v_ref, vt_ref, facts[0][0])
    fill_values(far_v_ref, far_vt_ref, facts[1][0])
    caches = (
        (keys_ref, vt_ref, s_ref, p_ref) + facts[0][1:],
        (far_keys_ref, far_vt_ref, far_s_ref, far_p_ref) + facts[1][1:],
    )

    def scores(head, slot):
        key = lax.broadcasted_iota(jnp.int32, (rows, rows), 0)
        row = lax.broadcasted_iota(jnp.int32, (rows, rows), 1)
        fresh = jnp.where(key <= row, scores_of(nk_ref[...], q_ref, head), MASKED)
        n_ref[slot] = fresh
        top = fold_max(fresh) * BASE_FACTOR
        for keys, _, kept_scores, _, factor, _ in caches:
            for at in range(0, slots, CHUNK):
                cached = cache_scores(keys, q_ref, head, at)
                kept_scores[slot, at : at + CHUNK, :] = cached
                top = jnp.maximum(top, fold_max(cached) * factor)
        return top

    top = scores(0, 0)
    for head in range(GROUP):
        slot = head % 2
        peak = jnp.max(top, axis=0, keepdims=True)
        if head + 1 < GROUP:
            top = scores(head + 1, 1 - slot)
        pn_ref[slot] = jnp.exp2(n_ref[slot] * BASE_FACTOR - peak).astype(jnp.bfloat16)
        summed = jnp.dot(nvt_ref[...], pn_ref[slot], preferred_element_type=jnp.float32)
        acc, total = summed[:HD], summed[HD : HD + 1]
        for _, values, kept_scores, weights, factor, value_scale in caches:
            for at in range(0, slots, CHUNK):
                weights[slot, at : at + CHUNK, :] = jnp.exp2(
                    kept_scores[slot, at : at + CHUNK, :] * factor - peak
                ).astype(jnp.bfloat16)
            summed = jnp.dot(values[...], weights[slot], preferred_element_type=jnp.float32)
            acc += value_scale * summed[:HD]
            total += summed[HD : HD + 1]
        acc_ref[head * HD : (head + 1) * HD, :] = acc
        total_ref[head : head + 1, :] = total
        peak_ref[head : head + 1, :] = peak


def last_weights_kernel(
    live_ref, scale_ref, q_ref, nk_ref, k_ref, peak_in, weights_ref, kept_ref, s_ref, keys_ref, *, distance
):
    slots = k_ref.shape[0]
    live, factor, _ = facts_at(live_ref, scale_ref, distance)
    fill_keys(k_ref, nk_ref, live, keys_ref)

    def scores(head, slot):
        top = None
        for at in range(0, slots, CHUNK):
            cached = cache_scores(keys_ref, q_ref, head, at)
            s_ref[slot, at : at + CHUNK, :] = cached
            top = fold_max(cached) if top is None else jnp.maximum(top, fold_max(cached))
        return top

    top = scores(0, 0)
    for head in range(GROUP):
        slot = head % 2
        before = peak_in[head : head + 1, :]
        peak = jnp.maximum(before, jnp.max(top, axis=0, keepdims=True) * factor)
        kept_ref[head : head + 1, :] = jnp.exp2(before - peak)
        if head + 1 < GROUP:
            top = scores(head + 1, 1 - slot)
        for at in range(0, slots, CHUNK):
            weights_ref[head * slots + at : head * slots + at + CHUNK, :] = jnp.exp2(
                s_ref[slot, at : at + CHUNK, :] * factor - peak
            ).astype(jnp.bfloat16)


def row_plan(head_axis):
    index = lax.axis_index(head_axis)
    chip, core = index // 2, index % 2
    one, three = chip + 1 - 2 * (chip % 2), 3 - chip
    first = jnp.where(core == 0, one, three)
    second = jnp.where(core == 0, three, one)
    opposite = 3 - one
    return chip, core, first, second, opposite


def split_rows(turned_ref, send_ref, keep_ref):
    chip, core, first, second, opposite = row_plan("head")
    block = turned_ref.shape[0] // 8
    for out_ref, owner_core, chips in (
        (send_ref, 1 - core, (chip, first, second, opposite)),
        (keep_ref, core, (chip, second, first, opposite)),
    ):
        for at, owner in enumerate(chips):
            start = pl.multiple_of((2 * owner + owner_core) * block, block)
            out_ref[at * block : (at + 1) * block, :] = turned_ref[pl.ds(start, block), :]


def finish_kernel(
    live_ref, scale_ref, weights_ref, v_ref, acc_ref, kept_ref, total_ref,
    send_ref, keep_ref, vt_ref, turned_ref, *, distance,
):
    slots = v_ref.shape[0]
    live, _, value_scale = facts_at(live_ref, scale_ref, distance)
    fill_values(v_ref, vt_ref, live)
    for head in range(GROUP):
        summed = jnp.dot(
            vt_ref[...], weights_ref[head * slots : (head + 1) * slots, :],
            preferred_element_type=jnp.float32,
        )
        at = slice(head * HD, (head + 1) * HD)
        kept = kept_ref[head : head + 1, :]
        total = total_ref[head : head + 1, :] * kept + summed[HD : HD + 1]
        attended = (acc_ref[at, :] * kept + value_scale * summed[:HD]) / total
        turned_ref[:, at] = attended.T.astype(jnp.bfloat16)
    split_rows(turned_ref, send_ref, keep_ref)


def project_own_kernel(keep_ref, w_ref, out_ref):
    step = 512
    for at in range(0, out_ref.shape[1], step):
        columns = slice(at, at + step)
        out_ref[:, columns] = jnp.dot(keep_ref[...], w_ref[:, columns], preferred_element_type=jnp.float32)


def project_kernel(own_ref, got_ref, other_w_ref, send_out, keep_out, *, start):
    half, width = keep_out.shape
    step = 512
    for at in range(0, width, step):
        columns = slice(start + at, start + at + step)
        partial = own_ref[:, columns] + jnp.dot(
            got_ref[...], other_w_ref[:, columns], preferred_element_type=jnp.float32
        )
        keep_out[:, at : at + step] = partial[:half]
        send_out[:, at : at + step] = partial[half:].astype(jnp.bfloat16)


def params(mib):
    return pltpu.CompilerParams(vmem_limit_bytes=mib << 20)


def cost(keys, rows, products):
    wide = GROUP * rows * keys
    return pl.CostEstimate(flops=2 * products * wide * HD, transcendentals=wide, bytes_accessed=1 << 20)


def shifted(value, axis, steps):
    count = lax.axis_size(axis)
    return lax.ppermute(value, axis, [(i, i + steps) for i in range(count - steps)])


def core_pairs():
    return [(i, i ^ 1) for i in range(8)]


def chip_pairs(first):
    pairs = []
    for i in range(8):
        chip, core = i // 2, i % 2
        other = chip ^ 1 if (core == 0) == first else chip ^ 3
        pairs.append((i, 2 * other + core))
    return pairs


def on_device(
    queries, new_keys, new_values, cache_keys, cache_values, key_counts, scale_exps, out_weight
):
    rows = queries.shape[0]
    own_keys = cache_keys[0, 0]
    own_values = cache_values[0, 0]
    slots = own_keys.shape[0]
    exps = scale_exps.T
    wide = GROUP * HD
    f32, bf16 = jnp.float32, jnp.bfloat16

    keys_1 = shifted(own_keys, "section", 1)
    values_1 = shifted(own_values, "section", 1)
    other_weight = lax.ppermute(out_weight, "head", core_pairs())
    keys_2 = shifted(keys_1, "section", 1)
    values_2 = shifted(values_1, "section", 1)

    acc_shape = jax.ShapeDtypeStruct((wide, rows), f32)
    row_shape = jax.ShapeDtypeStruct((GROUP, rows), f32)
    vt = lambda n: pltpu.VMEM((HD + ONES_ROWS, n), bf16)
    pair = lambda n, t: pltpu.VMEM((2, n, rows), t)
    local = (key_counts, exps, queries, new_keys, new_values, own_keys, own_values)
    acc, peak, total, q, live, scale, near_keys = pl.pallas_call(
        near_kernel,
        out_shape=(
            acc_shape, row_shape, row_shape, jax.ShapeDtypeStruct(queries.shape, bf16),
            jax.ShapeDtypeStruct((GROUP, rows), jnp.int32), row_shape,
            jax.ShapeDtypeStruct(new_keys.shape, bf16),
        ),
        in_specs=[HBM] * 7 + [VMEM] * 2,
        out_specs=(VMEM,) * 7,
        scratch_shapes=[
            pltpu.SMEM(key_counts.shape, jnp.int32), pltpu.SMEM(exps.shape, jnp.int32),
            pltpu.VMEM(new_values.shape, bf16),
            pltpu.VMEM(own_keys.shape, bf16), pltpu.VMEM(own_values.shape, bf16),
            pltpu.VMEM(own_keys.shape, bf16), pltpu.VMEM(own_keys.shape, bf16),
            vt(slots), vt(slots), vt(rows),
            pair(slots, f32), pair(slots, f32), pair(rows, f32),
            pair(slots, bf16), pair(slots, bf16), pair(rows, bf16),
            pltpu.SemaphoreType.DMA((7,)),
        ],
        compiler_params=params(24),
        cost_estimate=cost(2 * slots + rows, rows, 2),
        name="near",
    )(*(pltpu.with_memory_space_constraint(value, pltpu.HBM) for value in local), keys_1, values_1)
    weights, kept = pl.pallas_call(
        functools.partial(last_weights_kernel, distance=2),
        out_shape=(jax.ShapeDtypeStruct((GROUP * slots, rows), bf16), row_shape),
        in_specs=[VMEM] * 6,
        out_specs=(VMEM, VMEM),
        scratch_shapes=[pair(slots, f32), pltpu.VMEM(own_keys.shape, bf16)],
        compiler_params=params(16),
        cost_estimate=cost(slots, rows, 1),
        name="last",
    )(live, scale, q, near_keys, keys_2, peak)

    half, quarter, eighth = rows // 2, rows // 4, rows // 8
    send, keep = pl.pallas_call(
        functools.partial(finish_kernel, distance=2),
        out_shape=(jax.ShapeDtypeStruct((half, wide), bf16),) * 2,
        in_specs=[VMEM] * 7,
        out_specs=(VMEM, VMEM),
        scratch_shapes=[vt(slots), pltpu.VMEM((rows, wide), bf16)],
        compiler_params=params(16),
        cost_estimate=cost(slots, rows, 1),
        name="finish",
    )(live, scale, weights, values_2, acc, kept, total)
    got = lax.ppermute(send, "head", core_pairs())
    own_share = pl.pallas_call(
        project_own_kernel,
        out_shape=jax.ShapeDtypeStruct((half, out_weight.shape[1]), f32),
        in_specs=[VMEM] * 2,
        out_specs=VMEM,
        compiler_params=params(16),
        cost_estimate=pl.CostEstimate(
            flops=2 * half * wide * out_weight.shape[1], transcendentals=0, bytes_accessed=1 << 20
        ),
        name="project_own",
    )(keep, out_weight)

    part = out_weight.shape[1] // 2
    size = lax.axis_size("section")
    pieces = []
    for start in (0, part):
        send, kept_rows = pl.pallas_call(
            functools.partial(project_kernel, start=start),
            out_shape=(jax.ShapeDtypeStruct((quarter, part), bf16), jax.ShapeDtypeStruct((quarter, part), f32)),
            in_specs=[VMEM] * 3,
            out_specs=(VMEM, VMEM),
            compiler_params=params(16),
            cost_estimate=pl.CostEstimate(
                flops=rows * wide * part, transcendentals=0, bytes_accessed=1 << 20
            ),
            name="project",
        )(own_share, got, other_weight)
        first = lax.ppermute(send, "head", chip_pairs(True))
        two = kept_rows + first.astype(f32)
        second = lax.ppermute(two[eighth:].astype(bf16), "head", chip_pairs(False))
        done = (two[:eighth] + second.astype(f32)).astype(bf16)
        pieces.append(lax.ppermute(done, "section", [(i, (i + 1) % size) for i in range(size)]))
    return jnp.concatenate(pieces, axis=1).astype(f32)


def solution(mesh):
    in_specs = (
        P("section", "head"),
        P("section", "head"),
        P("section", "head"),
        P("section", "head", None, None),
        P("section", "head", None, None),
        P(),
        P(),
        P("head", None),
    )
    out_specs = P(("section", "head"), None)
    return jax.shard_map(on_device, mesh=mesh, in_specs=in_specs, out_specs=out_specs, check_vma=False)
```

time: 74.4 us -> 72.2 us (0.970)
  waiting for transfers between devices: 19.3 us -> 17.5 us
  Pallas kernels: 12.6 us -> 11.6 us
    ppermute x1, waiting for transfers between devices: 1.14 us -> 0.01 us  [on_device(): got = lax.ppermute(send, 'head', core_pairs())]
    pallas_call x2, Pallas kernels: 2.56 us -> 1.45 us  [on_device(): pl.pallas_call(functools.partial(project_kernel, start=start), out_shape=...]
  transfers between devices with their start and end apart: 12 -> 12, of which waited for: 9 -> 8; matrix products, arithmetic and copies ran while one was open for 0% -> 0% of each run, Pallas kernels for 15% -> 15%
where the time goes in v2:
time: 72.2 us; the launch traced here: 71.5 us
  starting transfers between devices  41.2 us (57%)
  waiting for transfers between devices  17.5 us (24%)
  Pallas kernels  11.6 us (16%)
  other arithmetic  0.98 us (1%)
    ppermute x1, starting transfers between devices, on_device(): other_weight = lax.ppermute(out_weight, 'head', core_pairs())  12.6 us
    ppermute x2, waiting for transfers between devices, on_device(): lax.ppermute(done, 'section', [(i, (i + 1) % size) for i in range(size)])  11 us
    ppermute x4, starting transfers between devices, shifted(): lax.ppermute(value, axis, [(i, i + steps) for i in range(count - steps)])  10.6 us
    ppermute x2, starting transfers between devices, on_device(): first = lax.ppermute(send, 'head', chip_pairs(True))  6.49 us
    pallas_call x1, Pallas kernels, on_device(): pl.pallas_call(near_kernel, out_shape=(acc_shape, row_shape, row_shape, j...  6.37 us
    ppermute x2, starting transfers between devices, on_device(): second = lax.ppermute(two[eighth:].astype(bf16), 'head', chip_pairs(False))  4.49 us
    ppermute x2, starting transfers between devices, on_device(): lax.ppermute(done, 'section', [(i, (i + 1) % size) for i in range(size)])  3.84 us
    ppermute x4, waiting for transfers between devices, shifted(): lax.ppermute(value, axis, [(i, i + steps) for i in range(count - steps)])  3.45 us
  transfers between devices with their start and end apart: 12, of which 8 were waited for; matrix products, arithmetic and copies ran while one was open for 0% of the time, Pallas kernels for 15%

profile of v2, /device:TPU:1, one launch (start us, length us, event | category | flops | bytes accessed | tf_op | source)
XLA Modules:
  0.0 71.5 jit_solution(5616231390687806242)
XLA Ops:
  0.0 0.0 copy-start
  0.0 12.6 %collective-permute-start.5 = (bf16[1024,4096]{1,0:T(8,128)(2,1)}, bf16[1024,4096]{1,0:T(8,128)(2,1)S(1)}, u32[]{:S(2)}, u32[]{:S(2)}) collective-permute-start(bf16[1024,4096]{1,0:T(8,128)(2,1)} %w_ref.1), channel_id=1, source_target_pairs={{0,1},{1,0},{2,3},{3,2},{4,5},{5,4},{6,7},{7,6},{8,9},{9,8},{10,11... | collective-permute-start | bytes 25165832 | tf_op jit(solution)/shard_map/ppermute | solution.py:275
  12.6 1.3 %collective-permute-start = (bf16[768,128]{1,0:T(8,128)(2,1)}, bf16[768,128]{1,0:T(8,128)(2,1)S(1)}, u32[]{:S(2)}, u32[]{:S(2)}) collective-permute-start(bf16[768,128]{1,0:T(8,128)(2,1)} %bitcast.3), channel_id=1, source_target_pairs={{0,8},{8,16},{16,24},{24,32},{32,40},{40,48},{48,56},{56,64},{64,7... | collective-permute-start | bytes 589832 | tf_op jit(solution)/shard_map/ppermute | solution.py:246
  14.0 1.3 %collective-permute-start.1 = (bf16[768,128]{1,0:T(8,128)(2,1)}, bf16[768,128]{1,0:T(8,128)(2,1)S(1)}, u32[]{:S(2)}, u32[]{:S(2)}) collective-permute-start(bf16[768,128]{1,0:T(8,128)(2,1)} %bitcast.5), channel_id=1, source_target_pairs={{0,8},{8,16},{16,24},{24,32},{32,40},{40,48},{48,56},{56,64},{64,7... | collective-permute-start | bytes 589832 | tf_op jit(solution)/shard_map/ppermute | solution.py:246
  15.3 3.2 %collective-permute-done.far_k_ref = bf16[768,128]{1,0:T(8,128)(2,1)S(1)} collective-permute-done((bf16[768,128]{1,0:T(8,128)(2,1)}, bf16[768,128]{1,0:T(8,128)(2,1)S(1)}, u32[]{:S(2)}, u32[]{:S(2)}) %collective-permute-start) | collective-permute-done | bytes 196640 | tf_op jit(solution)/shard_map/ppermute | solution.py:246
  18.5 4.0 %collective-permute-start.2 = (bf16[768,128]{1,0:T(8,128)(2,1)S(1)}, bf16[768,128]{1,0:T(8,128)(2,1)S(1)}, u32[]{:S(2)}, u32[]{:S(2)}) collective-permute-start(bf16[768,128]{1,0:T(8,128)(2,1)S(1)} %collective-permute-done.far_k_ref), channel_id=1, source_target_pairs={{0,8},{8,16},{16,24},{24,32},{32,40},{40,48},{48,56},{56,64},{64,7... | collective-permute-start | bytes 589832 | tf_op jit(solution)/shard_map/ppermute | solution.py:246
  22.5 0.2 collective-permute-done.1.far_v_ref
  22.7 4.0 %collective-permute-start.3 = (bf16[768,128]{1,0:T(8,128)(2,1)S(1)}, bf16[768,128]{1,0:T(8,128)(2,1)S(1)}, u32[]{:S(2)}, u32[]{:S(2)}) collective-permute-start(bf16[768,128]{1,0:T(8,128)(2,1)S(1)} %collective-permute-done.1.far_v_ref), channel_id=1, source_target_pairs={{0,8},{8,16},{16,24},{24,32},{32,40},{40,48},{48,56},{56,64},{64,7... | collective-permute-start | bytes 589832 | tf_op jit(solution)/shard_map/ppermute | solution.py:246
  26.7 6.4 %near.1 = (f32[1024,256]{1,0:T(8,128)S(1)}, f32[8,256]{1,0:T(8,128)S(1)}, f32[8,256]{1,0:T(8,128)S(1)}, bf16[256,1024]{1,0:T(8,128)(2,1)S(1)}, s32[8,256]{1,0:T(...) custom-call(s32[96]{0:T(128)} %counts_hbm.1, s32[2,96]{1,0:T(2,128)} %bitcast.7, bf16[256,1024]{1,0:T(8,128)(2,1)} %q_hbm.1, ...), custom_call_target="tpu_custom_call" | custom-call | flops 1879048192 | bytes 1048576 | tf_op jit(solution)/shard_map/near/pallas_call | solution.py:284
  33.1 0.0 collective-permute-done.2.k_ref
  33.1 1.7 %last.1 = (bf16[6144,256]{1,0:T(8,128)(2,1)S(1)}, f32[8,256]{1,0:T(8,128)S(1)}) custom-call(s32[8,256]{1,0:T(8,128)S(1)} %get-tuple-element.20.live_ref, f32[8,256]{1,0:T(8,128)S(1)} %get-tuple-element.21.scale_ref, bf16[256,1024]{1,0:T(8,128)(2,1)S(1)} %get-tuple-element.22.q_ref, bf16[256,128]{1,0:T(8,128)(2,1)S(1)} %get-tuple-element.23.nk_ref, ...), custom_call_target="tpu_custom_call" | custom-call | flops 402653184 | bytes 1048576 | tf_op jit(solution)/shard_map/last/pallas_call | solution.py:307
  34.8 0.0 collective-permute-done.3.v_ref
  34.8 0.9 %finish.1 = (bf16[128,1024]{1,0:T(8,128)(2,1)S(1)}, bf16[128,1024]{1,0:T(8,128)(2,1)S(1)}) custom-call(s32[8,256]{1,0:T(8,128)S(1)} %get-tuple-element.20.live_ref, f32[8,256]{1,0:T(8,128)S(1)} %get-tuple-element.21.scale_ref, bf16[6144,256]{1,0:T(8,128)(2,1)S(1)} %get-tuple-element.25.weights_ref, bf16[768,128]{1,0:T(8,128)(2,1)S(1)} %collective-permute-done.3.v_ref, ...), custom_call_target="tpu_custom_call" | custom-call | flops 402653184 | bytes 1048576 | tf_op jit(solution)/shard_map/finish/pallas_call | solution.py:319
  35.7 3.1 %collective-permute-start.4 = (bf16[128,1024]{1,0:T(8,128)(2,1)S(1)}, bf16[128,1024]{1,0:T(8,128)(2,1)S(1)}, u32[]{:S(2)}, u32[]{:S(2)}) collective-permute-start(bf16[128,1024]{1,0:T(8,128)(2,1)S(1)} %get-tuple-element.30), channel_id=1, source_target_pairs={{0,1},{1,0},{2,3},{3,2},{4,5},{5,4},{6,7},{7,6},{8,9},{9,8},{10,11... | collective-permute-start | bytes 786440 | tf_op jit(solution)/shard_map/ppermute | solution.py:329
  38.8 0.0 copy-done
  38.8 1.3 %project_own.1.own_ref = f32[128,4096]{1,0:T(8,128)S(1)} custom-call(bf16[128,1024]{1,0:T(8,128)(2,1)S(1)} %get-tuple-element.29.keep_ref, bf16[1024,4096]{1,0:T(8,128)(2,1)S(1)} %copy-done), custom_call_target="tpu_custom_call" | custom-call | flops 1073741824 | bytes 1048576 | tf_op jit(solution)/shard_map/project_own/pallas_call | solution.py:330
  40.1 0.0 collective-permute-done.4.got_ref
  40.1 0.0 collective-permute-done.5.other_w_ref
  40.1 0.7 %project.2 = (bf16[64,2048]{1,0:T(8,128)(2,1)S(1)}, f32[64,2048]{1,0:T(8,128)S(1)}) custom-call(f32[128,4096]{1,0:T(8,128)S(1)} %project_own.1.own_ref, bf16[128,1024]{1,0:T(8,128)(2,1)S(1)} %collective-permute-done.4.got_ref, bf16[1024,4096]{1,0:T(8,128)(2,1)S(1)} %collective-permute-done.5.other_w_ref), custom_call_target="tpu_custom_call" | custom-call | flops 536870912 | bytes 1048576 | tf_op jit(solution)/shard_map/project/pallas_call | solution.py:346
  40.9 1.9 %collective-permute-start.6 = (bf16[64,2048]{1,0:T(8,128)(2,1)S(1)}, bf16[64,2048]{1,0:T(8,128)(2,1)S(1)}, u32[]{:S(2)}, u32[]{:S(2)}) collective-permute-start(bf16[64,2048]{1,0:T(8,128)(2,1)S(1)} %get-tuple-element.32), channel_id=1, source_target_pairs={{0,2},{1,7},{2,0},{3,5},{4,6},{5,3},{6,4},{7,1},{8,10},{9,15},{10,... | collective-permute-start | bytes 786440 | tf_op jit(solution)/shard_map/ppermute | solution.py:357
  42.8 0.7 %project.3 = (bf16[64,2048]{1,0:T(8,128)(2,1)S(1)}, f32[64,2048]{1,0:T(8,128)S(1)}) custom-call(f32[128,4096]{1,0:T(8,128)S(1)} %project_own.1.own_ref, bf16[128,1024]{1,0:T(8,128)(2,1)S(1)} %collective-permute-done.4.got_ref, bf16[1024,4096]{1,0:T(8,128)(2,1)S(1)} %collective-permute-done.5.other_w_ref), custom_call_target="tpu_custom_call" | custom-call | flops 536870912 | bytes 1048576 | tf_op jit(solution)/shard_map/project/pallas_call | solution.py:346
  43.5 4.6 %collective-permute-start.9 = (bf16[64,2048]{1,0:T(8,128)(2,1)S(1)}, bf16[64,2048]{1,0:T(8,128)(2,1)S(1)}, u32[]{:S(2)}, u32[]{:S(2)}) collective-permute-start(bf16[64,2048]{1,0:T(8,128)(2,1)S(1)} %get-tuple-element.34), channel_id=1, source_target_pairs={{0,2},{1,7},{2,0},{3,5},{4,6},{5,3},{6,4},{7,1},{8,10},{9,15},{10,... | collective-permute-start | bytes 786440 | tf_op jit(solution)/shard_map/ppermute | solution.py:357
  48.1 1.1 %collective-permute-done.6 = bf16[64,2048]{1,0:T(8,128)(2,1)S(1)} collective-permute-done((bf16[64,2048]{1,0:T(8,128)(2,1)S(1)}, bf16[64,2048]{1,0:T(8,128)(2,1)S(1)}, u32[]{:S(2)}, u32[]{:S(2)}) %collective-permute-start.6) | collective-permute-done | bytes 262176 | tf_op jit(solution)/shard_map/ppermute | solution.py:357
  49.3 1.9 %collective-permute-start.7 = (bf16[32,2048]{1,0:T(8,128)(2,1)S(1)}, bf16[32,2048]{1,0:T(8,128)(2,1)S(1)}, u32[]{:S(2)}, u32[]{:S(2)}) collective-permute-start(bf16[32,2048]{1,0:T(8,128)(2,1)S(1)} %slice.31), channel_id=1, source_target_pairs={{0,6},{1,3},{2,4},{3,1},{4,2},{5,7},{6,0},{7,5},{8,14},{9,11},{10,... | collective-permute-start | bytes 393224 | tf_op jit(solution)/shard_map/ppermute | solution.py:359
  51.2 0.8 %collective-permute-done.9 = bf16[64,2048]{1,0:T(8,128)(2,1)S(1)} collective-permute-done((bf16[64,2048]{1,0:T(8,128)(2,1)S(1)}, bf16[64,2048]{1,0:T(8,128)(2,1)S(1)}, u32[]{:S(2)}, u32[]{:S(2)}) %collective-permute-start.9) | collective-permute-done | bytes 262176 | tf_op jit(solution)/shard_map/ppermute | solution.py:357
  52.1 2.6 %collective-permute-start.10 = (bf16[32,2048]{1,0:T(8,128)(2,1)S(1)}, bf16[32,2048]{1,0:T(8,128)(2,1)S(1)}, u32[]{:S(2)}, u32[]{:S(2)}) collective-permute-start(bf16[32,2048]{1,0:T(8,128)(2,1)S(1)} %slice.30), channel_id=1, source_target_pairs={{0,6},{1,3},{2,4},{3,1},{4,2},{5,7},{6,0},{7,5},{8,14},{9,11},{10,... | collective-permute-start | bytes 393224 | tf_op jit(solution)/shard_map/ppermute | solution.py:359
  54.6 0.3 collective-permute-done.7
  55.0 1.9 %collective-permute-start.8 = (bf16[32,2048]{1,0:T(8,128)(2,1)S(1)}, bf16[32,2048]{1,0:T(8,128)(2,1)S(1)}, u32[]{:S(2)}, u32[]{:S(2)}) collective-permute-start(bf16[32,2048]{1,0:T(8,128)(2,1)S(1)} %fusion.1), channel_id=1, source_target_pairs={{0,8},{8,16},{16,24},{24,32},{32,40},{40,48},{48,56},{56,64},{64,7... | collective-permute-start | bytes 393224 | tf_op jit(solution)/shard_map/ppermute | solution.py:361
  56.9 0.8 %collective-permute-done.10 = bf16[32,2048]{1,0:T(8,128)(2,1)S(1)} collective-permute-done((bf16[32,2048]{1,0:T(8,128)(2,1)S(1)}, bf16[32,2048]{1,0:T(8,128)(2,1)S(1)}, u32[]{:S(2)}, u32[]{:S(2)}) %collective-permute-start.10) | collective-permute-done | bytes 131104 | tf_op jit(solution)/shard_map/ppermute | solution.py:359
  57.8 1.9 %collective-permute-start.11 = (bf16[32,2048]{1,0:T(8,128)(2,1)S(1)}, bf16[32,2048]{1,0:T(8,128)(2,1)S(1)}, u32[]{:S(2)}, u32[]{:S(2)}) collective-permute-start(bf16[32,2048]{1,0:T(8,128)(2,1)S(1)} %fusion), channel_id=1, source_target_pairs={{0,8},{8,16},{16,24},{24,32},{32,40},{40,48},{48,56},{56,64},{64,7... | collective-permute-start | bytes 393224 | tf_op jit(solution)/shard_map/ppermute | solution.py:361
  59.7 7.2 %collective-permute-done.8 = bf16[32,2048]{1,0:T(8,128)(2,1)S(1)} collective-permute-done((bf16[32,2048]{1,0:T(8,128)(2,1)S(1)}, bf16[32,2048]{1,0:T(8,128)(2,1)S(1)}, u32[]{:S(2)}, u32[]{:S(2)}) %collective-permute-start.8) | collective-permute-done | bytes 131104 | tf_op jit(solution)/shard_map/ppermute | solution.py:361
  66.9 3.8 %collective-permute-done.11 = bf16[32,2048]{1,0:T(8,128)(2,1)S(1)} collective-permute-done((bf16[32,2048]{1,0:T(8,128)(2,1)S(1)}, bf16[32,2048]{1,0:T(8,128)(2,1)S(1)}, u32[]{:S(2)}, u32[]{:S(2)}) %collective-permute-start.11) | collective-permute-done | bytes 131104 | tf_op jit(solution)/shard_map/ppermute | solution.py:361
  70.7 0.8 %maximum_convert_fusion = f32[32,4096]{1,0:T(8,128)} fusion(bf16[32,2048]{1,0:T(8,128)(2,1)S(1)} %collective-permute-done.11, bf16[32,2048]{1,0:T(8,128)(2,1)S(1)} %collective-permute-done.8), kind=kLoop, calls=%fused_computation.8 | loop fusion | flops 524288 | bytes 786432 | tf_op jit(solution)/shard_map/convert_element_type | solution.py:362
  (6 shorter events, 0.2 us)
Async XLA Ops:
  0.0 38.8 %copy-start = (bf16[1024,4096]{1,0:T(8,128)(2,1)S(1)}, bf16[1024,4096]{1,0:T(8,128)(2,1)}, u32[]{:S(2)}) copy-start(bf16[1024,4096]{1,0:T(8,128)(2,1)} %w_ref.1) | copy-start | bytes 25165828
  0.0 40.1 %collective-permute-start.5 = (bf16[1024,4096]{1,0:T(8,128)(2,1)}, bf16[1024,4096]{1,0:T(8,128)(2,1)S(1)}, u32[]{:S(2)}, u32[]{:S(2)}) collective-permute-start(bf16[1024,4096]{1,0:T(8,128)(2,1)} %w_ref.1), channel_id=1, source_target_pairs={{0,1},{1,0},{2,3},{3,2},{4,5},{5,4},{6,7},{7,6},{8,9},{9,8},{10,11... | collective-permute-start | bytes 25165832 | tf_op jit(solution)/shard_map/ppermute | solution.py:275
  12.6 5.9 %collective-permute-start = (bf16[768,128]{1,0:T(8,128)(2,1)}, bf16[768,128]{1,0:T(8,128)(2,1)S(1)}, u32[]{:S(2)}, u32[]{:S(2)}) collective-permute-start(bf16[768,128]{1,0:T(8,128)(2,1)} %bitcast.3), channel_id=1, source_target_pairs={{0,8},{8,16},{16,24},{24,32},{32,40},{40,48},{48,56},{56,64},{64,7... | collective-permute-start | bytes 589832 | tf_op jit(solution)/shard_map/ppermute | solution.py:246
  14.0 8.8 %collective-permute-start.1 = (bf16[768,128]{1,0:T(8,128)(2,1)}, bf16[768,128]{1,0:T(8,128)(2,1)S(1)}, u32[]{:S(2)}, u32[]{:S(2)}) collective-permute-start(bf16[768,128]{1,0:T(8,128)(2,1)} %bitcast.5), channel_id=1, source_target_pairs={{0,8},{8,16},{16,24},{24,32},{32,40},{40,48},{48,56},{56,64},{64,7... | collective-permute-start | bytes 589832 | tf_op jit(solution)/shard_map/ppermute | solution.py:246
  18.5 14.6 %collective-permute-start.2 = (bf16[768,128]{1,0:T(8,128)(2,1)S(1)}, bf16[768,128]{1,0:T(8,128)(2,1)S(1)}, u32[]{:S(2)}, u32[]{:S(2)}) collective-permute-start(bf16[768,128]{1,0:T(8,128)(2,1)S(1)} %collective-permute-done.far_k_ref), channel_id=1, source_target_pairs={{0,8},{8,16},{16,24},{24,32},{32,40},{40,48},{48,56},{56,64},{64,7... | collective-permute-start | bytes 589832 | tf_op jit(solution)/shard_map/ppermute | solution.py:246
  22.7 12.1 %collective-permute-start.3 = (bf16[768,128]{1,0:T(8,128)(2,1)S(1)}, bf16[768,128]{1,0:T(8,128)(2,1)S(1)}, u32[]{:S(2)}, u32[]{:S(2)}) collective-permute-start(bf16[768,128]{1,0:T(8,128)(2,1)S(1)} %collective-permute-done.1.far_v_ref), channel_id=1, source_target_pairs={{0,8},{8,16},{16,24},{24,32},{32,40},{40,48},{48,56},{56,64},{64,7... | collective-permute-start | bytes 589832 | tf_op jit(solution)/shard_map/ppermute | solution.py:246
  35.7 4.4 %collective-permute-start.4 = (bf16[128,1024]{1,0:T(8,128)(2,1)S(1)}, bf16[128,1024]{1,0:T(8,128)(2,1)S(1)}, u32[]{:S(2)}, u32[]{:S(2)}) collective-permute-start(bf16[128,1024]{1,0:T(8,128)(2,1)S(1)} %get-tuple-element.30), channel_id=1, source_target_pairs={{0,1},{1,0},{2,3},{3,2},{4,5},{5,4},{6,7},{7,6},{8,9},{9,8},{10,11... | collective-permute-start | bytes 786440 | tf_op jit(solution)/shard_map/ppermute | solution.py:329
  40.9 8.3 %collective-permute-start.6 = (bf16[64,2048]{1,0:T(8,128)(2,1)S(1)}, bf16[64,2048]{1,0:T(8,128)(2,1)S(1)}, u32[]{:S(2)}, u32[]{:S(2)}) collective-permute-start(bf16[64,2048]{1,0:T(8,128)(2,1)S(1)} %get-tuple-element.32), channel_id=1, source_target_pairs={{0,2},{1,7},{2,0},{3,5},{4,6},{5,3},{6,4},{7,1},{8,10},{9,15},{10,... | collective-permute-start | bytes 786440 | tf_op jit(solution)/shard_map/ppermute | solution.py:357
  43.5 8.5 %collective-permute-start.9 = (bf16[64,2048]{1,0:T(8,128)(2,1)S(1)}, bf16[64,2048]{1,0:T(8,128)(2,1)S(1)}, u32[]{:S(2)}, u32[]{:S(2)}) collective-permute-start(bf16[64,2048]{1,0:T(8,128)(2,1)S(1)} %get-tuple-element.34), channel_id=1, source_target_pairs={{0,2},{1,7},{2,0},{3,5},{4,6},{5,3},{6,4},{7,1},{8,10},{9,15},{10,... | collective-permute-start | bytes 786440 | tf_op jit(solution)/shard_map/ppermute | solution.py:357
  49.3 5.7 %collective-permute-start.7 = (bf16[32,2048]{1,0:T(8,128)(2,1)S(1)}, bf16[32,2048]{1,0:T(8,128)(2,1)S(1)}, u32[]{:S(2)}, u32[]{:S(2)}) collective-permute-start(bf16[32,2048]{1,0:T(8,128)(2,1)S(1)} %slice.31), channel_id=1, source_target_pairs={{0,6},{1,3},{2,4},{3,1},{4,2},{5,7},{6,0},{7,5},{8,14},{9,11},{10,... | collective-permute-start | bytes 393224 | tf_op jit(solution)/shard_map/ppermute | solution.py:359
  52.1 5.7 %collective-permute-start.10 = (bf16[32,2048]{1,0:T(8,128)(2,1)S(1)}, bf16[32,2048]{1,0:T(8,128)(2,1)S(1)}, u32[]{:S(2)}, u32[]{:S(2)}) collective-permute-start(bf16[32,2048]{1,0:T(8,128)(2,1)S(1)} %slice.30), channel_id=1, source_target_pairs={{0,6},{1,3},{2,4},{3,1},{4,2},{5,7},{6,0},{7,5},{8,14},{9,11},{10,... | collective-permute-start | bytes 393224 | tf_op jit(solution)/shard_map/ppermute | solution.py:359
  55.0 11.9 %collective-permute-start.8 = (bf16[32,2048]{1,0:T(8,128)(2,1)S(1)}, bf16[32,2048]{1,0:T(8,128)(2,1)S(1)}, u32[]{:S(2)}, u32[]{:S(2)}) collective-permute-start(bf16[32,2048]{1,0:T(8,128)(2,1)S(1)} %fusion.1), channel_id=1, source_target_pairs={{0,8},{8,16},{16,24},{24,32},{32,40},{40,48},{48,56},{56,64},{64,7... | collective-permute-start | bytes 393224 | tf_op jit(solution)/shard_map/ppermute | solution.py:361
  57.8 12.9 %collective-permute-start.11 = (bf16[32,2048]{1,0:T(8,128)(2,1)S(1)}, bf16[32,2048]{1,0:T(8,128)(2,1)S(1)}, u32[]{:S(2)}, u32[]{:S(2)}) collective-permute-start(bf16[32,2048]{1,0:T(8,128)(2,1)S(1)} %fusion), channel_id=1, source_target_pairs={{0,8},{8,16},{16,24},{24,32},{32,40},{40,48},{48,56},{56,64},{64,7... | collective-permute-start | bytes 393224 | tf_op jit(solution)/shard_map/ppermute | solution.py:361

commit v3 on v2

--- a/solution.py
+++ b/solution.py
@@ -75,32 +75,39 @@
     vt_ref[HD:, :] = ones.astype(jnp.bfloat16)
 
 
-def near_kernel(
-    counts_hbm, exps_hbm, q_hbm, nk_hbm, nv_hbm, k_hbm, v_hbm, far_k_ref, far_v_ref,
-    acc_ref, peak_ref, total_ref, q_ref, live_ref, scale_ref, nk_ref,
-    counts_ref, exps_ref, nv_ref, k_ref, v_ref, keys_ref, far_keys_ref,
-    vt_ref, far_vt_ref, nvt_ref, s_ref, far_s_ref, n_ref, p_ref, far_p_ref, pn_ref, sems,
+def prepare_kernel(
+    counts_hbm, exps_hbm, q_hbm, nk_hbm, nv_hbm, k_hbm, v_hbm,
+    q_ref, live_ref, scale_ref, nk_ref, keys_ref, vt_ref, nvt_ref,
+    counts_ref, exps_ref, nv_ref, k_ref, v_ref, sems,
 ):
     pairs = (
-        (q_hbm, q_ref), (counts_hbm, counts_ref), (exps_hbm, exps_ref), (nk_hbm, nk_ref),
-        (k_hbm, k_ref), (nv_hbm, nv_ref), (v_hbm, v_ref),
+        (counts_hbm, counts_ref), (exps_hbm, exps_ref), (nk_hbm, nk_ref), (k_hbm, k_ref),
+        (nv_hbm, nv_ref), (v_hbm, v_ref), (q_hbm, q_ref),
     )
     copies = [pltpu.make_async_copy(source, target, sems.at[n]) for n, (source, target) in enumerate(pairs)]
     for copy in copies:
         copy.start()
     for copy in copies:
         copy.wait()
-    rows = q_ref.shape[0]
-    slots = k_ref.shape[0]
-    facts = [cache_facts(counts_ref, exps_ref, distance, rows) for distance in range(3)]
+    facts = [cache_facts(counts_ref, exps_ref, distance, q_ref.shape[0]) for distance in range(3)]
     for distance, (live, factor, value_scale) in enumerate(facts):
         live_ref[distance : distance + 1, :] = live
         scale_ref[2 * distance : 2 * distance + 1, :] = factor
         scale_ref[2 * distance + 1 : 2 * distance + 2, :] = value_scale
     fill_keys(k_ref, nk_ref, facts[0][0], keys_ref)
-    fill_keys(far_k_ref, nk_ref, facts[1][0], far_keys_ref)
     fill_values(nv_ref, nvt_ref)
     fill_values(v_ref, vt_ref, facts[0][0])
+
+
+def near_kernel(
+    q_ref, live_ref, scale_ref, nk_ref, keys_ref, vt_ref, nvt_ref, far_k_ref, far_v_ref,
+    acc_ref, peak_ref, total_ref,
+    far_keys_ref, far_vt_ref, s_ref, far_s_ref, n_ref, p_ref, far_p_ref, pn_ref,
+):
+    rows = q_ref.shape[0]
+    slots = far_k_ref.shape[0]
+    facts = [facts_at(live_ref, scale_ref, distance) for distance in range(2)]
+    fill_keys(far_k_ref, nk_ref, facts[1][0], far_keys_ref)
     fill_values(far_v_ref, far_vt_ref, facts[1][0])
     caches = (
         (keys_ref, vt_ref, s_ref, p_ref) + facts[0][1:],
@@ -281,29 +288,39 @@
     vt = lambda n: pltpu.VMEM((HD + ONES_ROWS, n), bf16)
     pair = lambda n, t: pltpu.VMEM((2, n, rows), t)
     local = (key_counts, exps, queries, new_keys, new_values, own_keys, own_values)
-    acc, peak, total, q, live, scale, near_keys = pl.pallas_call(
-        near_kernel,
+    like = lambda *shape: jax.ShapeDtypeStruct(shape, bf16)
+    ready = pl.pallas_call(
+        prepare_kernel,
         out_shape=(
-            acc_shape, row_shape, row_shape, jax.ShapeDtypeStruct(queries.shape, bf16),
-            jax.ShapeDtypeStruct((GROUP, rows), jnp.int32), row_shape,
-            jax.ShapeDtypeStruct(new_keys.shape, bf16),
+            like(*queries.shape), jax.ShapeDtypeStruct((GROUP, rows), jnp.int32), row_shape,
+            like(*new_keys.shape), like(*own_keys.shape), like(HD + ONES_ROWS, slots), like(HD + ONES_ROWS, rows),
         ),
-        in_specs=[HBM] * 7 + [VMEM] * 2,
+        in_specs=[HBM] * 7,
         out_specs=(VMEM,) * 7,
         scratch_shapes=[
             pltpu.SMEM(key_counts.shape, jnp.int32), pltpu.SMEM(exps.shape, jnp.int32),
-            pltpu.VMEM(new_values.shape, bf16),
-            pltpu.VMEM(own_keys.shape, bf16), pltpu.VMEM(own_values.shape, bf16),
-            pltpu.VMEM(own_keys.shape, bf16), pltpu.VMEM(own_keys.shape, bf16),
-            vt(slots), vt(slots), vt(rows),
+            pltpu.VMEM(new_values.shape, bf16), pltpu.VMEM(own_keys.shape, bf16),
+            pltpu.VMEM(own_values.shape, bf16), pltpu.SemaphoreType.DMA((7,)),
+        ],
+        compiler_params=params(8),
+        cost_estimate=pl.CostEstimate(flops=1 << 20, transcendentals=0, bytes_accessed=1 << 20),
+        name="prepare",
+    )(*(pltpu.with_memory_space_constraint(value, pltpu.HBM) for value in local))
+    q, live, scale, near_keys = ready[:4]
+    acc, peak, total = pl.pallas_call(
+        near_kernel,
+        out_shape=(acc_shape, row_shape, row_shape),
+        in_specs=[VMEM] * 9,
+        out_specs=(VMEM,) * 3,
+        scratch_shapes=[
+            pltpu.VMEM(own_keys.shape, bf16), vt(slots),
             pair(slots, f32), pair(slots, f32), pair(rows, f32),
             pair(slots, bf16), pair(slots, bf16), pair(rows, bf16),
-            pltpu.SemaphoreType.DMA((7,)),
         ],
         compiler_params=params(24),
         cost_estimate=cost(2 * slots + rows, rows, 2),
         name="near",
-    )(*(pltpu.with_memory_space_constraint(value, pltpu.HBM) for value in local), keys_1, values_1)
+    )(*ready, keys_1, values_1)
     weights, kept = pl.pallas_call(
         functools.partial(last_weights_kernel, distance=2),
         out_shape=(jax.ShapeDtypeStruct((GROUP * slots, rows), bf16), row_shape),

time: 72.2 us -> 70.9 us (0.982)
  starting transfers between devices: 41.2 us -> 39.5 us
    ppermute x4, starting transfers between devices: 10.6 us -> 9.26 us  [shifted(): lax.ppermute(value, axis, [(i, i + steps) for i in range(count - steps)])]
    pallas_call x1 -> x2, Pallas kernels: 6.37 us -> 6.45 us  [the longest x1 4.92 us: on_device(): pl.pallas_call(near_kernel, out_shape=(acc_shape, row_shape, row_shape),...]
  transfers between devices with their start and end apart: 12 -> 12, of which waited for: 8 -> 7; matrix products, arithmetic and copies ran while one was open for 0% -> 0% of each run, Pallas kernels for 15% -> 16%
where the time goes in v3:
time: 70.9 us; the launch traced here: 70.2 us
  starting transfers between devices  39.5 us (56%)
  waiting for transfers between devices  17.7 us (25%)
  Pallas kernels  11.7 us (17%)
  other arithmetic  0.98 us (1%)
    ppermute x1, starting transfers between devices, on_device(): other_weight = lax.ppermute(out_weight, 'head', core_pairs())  12.6 us
    ppermute x2, waiting for transfers between devices, on_device(): lax.ppermute(done, 'section', [(i, (i + 1) % size) for i in range(size)])  11.2 us
    ppermute x4, starting transfers between devices, shifted(): lax.ppermute(value, axis, [(i, i + steps) for i in range(count - steps)])  9.26 us
    ppermute x2, starting transfers between devices, on_device(): first = lax.ppermute(send, 'head', chip_pairs(True))  6.49 us
    pallas_call x1, Pallas kernels, on_device(): pl.pallas_call(near_kernel, out_shape=(acc_shape, row_shape, row_shape),...  4.92 us
    ppermute x2, starting transfers between devices, on_device(): second = lax.ppermute(two[eighth:].astype(bf16), 'head', chip_pairs(False))  4.49 us
    ppermute x2, starting transfers between devices, on_device(): lax.ppermute(done, 'section', [(i, (i + 1) % size) for i in range(size)])  3.84 us
    ppermute x4, waiting for transfers between devices, shifted(): lax.ppermute(value, axis, [(i, i + steps) for i in range(count - steps)])  3.51 us
  transfers between devices with their start and end apart: 12, of which 7 were waited for; matrix products, arithmetic and copies ran while one was open for 0% of the time, Pallas kernels for 16%

profile of v3, /device:TPU:1, one launch (start us, length us, event | category | flops | bytes accessed | tf_op | source)
XLA Modules:
  0.0 70.2 jit_solution(7888250853454908193)
XLA Ops:
  0.0 0.0 slice-start
  0.0 12.6 %collective-permute-start.5 = (bf16[1024,4096]{1,0:T(8,128)(2,1)}, bf16[1024,4096]{1,0:T(8,128)(2,1)S(1)}, u32[]{:S(2)}, u32[]{:S(2)}) collective-permute-start(bf16[1024,4096]{1,0:T(8,128)(2,1)} %w_ref.1), channel_id=1, source_target_pairs={{0,1},{1,0},{2,3},{3,2},{4,5},{5,4},{6,7},{7,6},{8,9},{9,8},{10,11... | collective-permute-start | bytes 25165832 | tf_op jit(solution)/shard_map/ppermute | solution.py:282
  12.6 1.3 %collective-permute-start = (bf16[768,128]{1,0:T(8,128)(2,1)}, bf16[768,128]{1,0:T(8,128)(2,1)S(1)}, u32[]{:S(2)}, u32[]{:S(2)}) collective-permute-start(bf16[768,128]{1,0:T(8,128)(2,1)} %bitcast.5), channel_id=1, source_target_pairs={{0,8},{8,16},{16,24},{24,32},{32,40},{40,48},{48,56},{56,64},{64,7... | collective-permute-start | bytes 589832 | tf_op jit(solution)/shard_map/ppermute | solution.py:253
  14.0 1.3 %collective-permute-start.2 = (bf16[768,128]{1,0:T(8,128)(2,1)}, bf16[768,128]{1,0:T(8,128)(2,1)S(1)}, u32[]{:S(2)}, u32[]{:S(2)}) collective-permute-start(bf16[768,128]{1,0:T(8,128)(2,1)} %bitcast.7), channel_id=1, source_target_pairs={{0,8},{8,16},{16,24},{24,32},{32,40},{40,48},{48,56},{56,64},{64,7... | collective-permute-start | bytes 589832 | tf_op jit(solution)/shard_map/ppermute | solution.py:253
  15.3 3.5 %collective-permute-done.far_k_ref = bf16[768,128]{1,0:T(8,128)(2,1)S(1)} collective-permute-done((bf16[768,128]{1,0:T(8,128)(2,1)}, bf16[768,128]{1,0:T(8,128)(2,1)S(1)}, u32[]{:S(2)}, u32[]{:S(2)}) %collective-permute-start) | collective-permute-done | bytes 196640 | tf_op jit(solution)/shard_map/ppermute | solution.py:253
  18.8 4.0 %collective-permute-start.1 = (bf16[768,128]{1,0:T(8,128)(2,1)S(1)}, bf16[768,128]{1,0:T(8,128)(2,1)S(1)}, u32[]{:S(2)}, u32[]{:S(2)}) collective-permute-start(bf16[768,128]{1,0:T(8,128)(2,1)S(1)} %collective-permute-done.far_k_ref), channel_id=1, source_target_pairs={{0,8},{8,16},{16,24},{24,32},{32,40},{40,48},{48,56},{56,64},{64,7... | collective-permute-start | bytes 589832 | tf_op jit(solution)/shard_map/ppermute | solution.py:253
  22.8 1.5 %prepare.1 = (bf16[256,1024]{1,0:T(8,128)(2,1)S(1)}, s32[8,256]{1,0:T(8,128)S(1)}, f32[8,256]{1,0:T(8,128)S(1)}, bf16[256,128]{1,0:T(8,128)(2,1)S(1)}, bf16[768,...) custom-call(s32[96]{0:T(128)} %counts_hbm.1, s32[2,96]{1,0:T(2,128)} %bitcast.9, ...), custom_call_target="tpu_custom_call" | custom-call | flops 1048576 | bytes 1048576 | tf_op jit(solution)/shard_map/prepare/pallas_call | solution.py:292
  24.3 0.0 collective-permute-done.2.far_v_ref
  24.3 2.7 %collective-permute-start.3 = (bf16[768,128]{1,0:T(8,128)(2,1)S(1)}, bf16[768,128]{1,0:T(8,128)(2,1)S(1)}, u32[]{:S(2)}, u32[]{:S(2)}) collective-permute-start(bf16[768,128]{1,0:T(8,128)(2,1)S(1)} %collective-permute-done.2.far_v_ref), channel_id=1, source_target_pairs={{0,8},{8,16},{16,24},{24,32},{32,40},{40,48},{48,56},{56,64},{64,7... | collective-permute-start | bytes 589832 | tf_op jit(solution)/shard_map/ppermute | solution.py:253
  27.0 0.0 slice-start.1
  27.0 4.9 %near.1 = (f32[1024,256]{1,0:T(8,128)S(1)}, f32[8,256]{1,0:T(8,128)S(1)}, f32[8,256]{1,0:T(8,128)S(1)}) custom-call(bf16[256,1024]{1,0:T(8,128)(2,1)S(1)} %get-tuple-element.25.q_ref, s32[8,256]{1,0:T(8,128)S(1)} %get-tuple-element.23.live_ref, f32[8,256]{1,0:T(8,128)S(1)} %get-tuple-element.24.scale_ref, bf16[256,128]{1,0:T(8,128)(2,1)S(1)} %get-tuple-element.26.nk_ref, ...), custom_call_target="tpu_custom_call" | custom-call | flops 1879048192 | bytes 1048576 | tf_op jit(solution)/shard_map/near/pallas_call | solution.py:310
  31.9 0.0 collective-permute-done.1.k_ref
  31.9 1.7 %last.1 = (bf16[6144,256]{1,0:T(8,128)(2,1)S(1)}, f32[8,256]{1,0:T(8,128)S(1)}) custom-call(s32[8,256]{1,0:T(8,128)S(1)} %get-tuple-element.23.live_ref, f32[8,256]{1,0:T(8,128)S(1)} %get-tuple-element.24.scale_ref, bf16[256,1024]{1,0:T(8,128)(2,1)S(1)} %get-tuple-element.25.q_ref, bf16[256,128]{1,0:T(8,128)(2,1)S(1)} %get-tuple-element.26.nk_ref, ...), custom_call_target="tpu_custom_call" | custom-call | flops 402653184 | bytes 1048576 | tf_op jit(solution)/shard_map/last/pallas_call | solution.py:324
  33.6 0.0 collective-permute-done.3.v_ref
  33.6 0.8 %finish.1 = (bf16[128,1024]{1,0:T(8,128)(2,1)S(1)}, bf16[128,1024]{1,0:T(8,128)(2,1)S(1)}) custom-call(s32[8,256]{1,0:T(8,128)S(1)} %get-tuple-element.23.live_ref, f32[8,256]{1,0:T(8,128)S(1)} %get-tuple-element.24.scale_ref, bf16[6144,256]{1,0:T(8,128)(2,1)S(1)} %get-tuple-element.31.weights_ref, bf16[768,128]{1,0:T(8,128)(2,1)S(1)} %collective-permute-done.3.v_ref, ...), custom_call_target="tpu_custom_call" | custom-call | flops 402653184 | bytes 1048576 | tf_op jit(solution)/shard_map/finish/pallas_call | solution.py:336
  34.5 2.8 %collective-permute-start.4 = (bf16[128,1024]{1,0:T(8,128)(2,1)S(1)}, bf16[128,1024]{1,0:T(8,128)(2,1)S(1)}, u32[]{:S(2)}, u32[]{:S(2)}) collective-permute-start(bf16[128,1024]{1,0:T(8,128)(2,1)S(1)} %get-tuple-element.36), channel_id=1, source_target_pairs={{0,1},{1,0},{2,3},{3,2},{4,5},{5,4},{6,7},{7,6},{8,9},{9,8},{10,11... | collective-permute-start | bytes 786440 | tf_op jit(solution)/shard_map/ppermute | solution.py:346
  37.3 0.0 slice-done
  37.3 0.0 slice-done.1
  37.3 1.3 %project_own.1.own_ref = f32[128,4096]{1,0:T(8,128)S(1)} custom-call(bf16[128,1024]{1,0:T(8,128)(2,1)S(1)} %get-tuple-element.35.keep_ref, bf16[1024,4096]{1,0:T(8,128)(2,1)S(1)} %bitcast.4), custom_call_target="tpu_custom_call" | custom-call | flops 1073741824 | bytes 1048576 | tf_op jit(solution)/shard_map/project_own/pallas_call | solution.py:347
  38.6 0.0 collective-permute-done.4.got_ref
  38.6 0.0 collective-permute-done.5.other_w_ref
  38.6 0.7 %project.2 = (bf16[64,2048]{1,0:T(8,128)(2,1)S(1)}, f32[64,2048]{1,0:T(8,128)S(1)}) custom-call(f32[128,4096]{1,0:T(8,128)S(1)} %project_own.1.own_ref, bf16[128,1024]{1,0:T(8,128)(2,1)S(1)} %collective-permute-done.4.got_ref, bf16[1024,4096]{1,0:T(8,128)(2,1)S(1)} %collective-permute-done.5.other_w_ref), custom_call_target="tpu_custom_call" | custom-call | flops 536870912 | bytes 1048576 | tf_op jit(solution)/shard_map/project/pallas_call | solution.py:363
  39.3 1.9 %collective-permute-start.6 = (bf16[64,2048]{1,0:T(8,128)(2,1)S(1)}, bf16[64,2048]{1,0:T(8,128)(2,1)S(1)}, u32[]{:S(2)}, u32[]{:S(2)}) collective-permute-start(bf16[64,2048]{1,0:T(8,128)(2,1)S(1)} %get-tuple-element.38), channel_id=1, source_target_pairs={{0,2},{1,7},{2,0},{3,5},{4,6},{5,3},{6,4},{7,1},{8,10},{9,15},{10,... | collective-permute-start | bytes 786440 | tf_op jit(solution)/shard_map/ppermute | solution.py:374
  41.3 0.7 %project.3 = (bf16[64,2048]{1,0:T(8,128)(2,1)S(1)}, f32[64,2048]{1,0:T(8,128)S(1)}) custom-call(f32[128,4096]{1,0:T(8,128)S(1)} %project_own.1.own_ref, bf16[128,1024]{1,0:T(8,128)(2,1)S(1)} %collective-permute-done.4.got_ref, bf16[1024,4096]{1,0:T(8,128)(2,1)S(1)} %collective-permute-done.5.other_w_ref), custom_call_target="tpu_custom_call" | custom-call | flops 536870912 | bytes 1048576 | tf_op jit(solution)/shard_map/project/pallas_call | solution.py:363
  42.0 4.6 %collective-permute-start.9 = (bf16[64,2048]{1,0:T(8,128)(2,1)S(1)}, bf16[64,2048]{1,0:T(8,128)(2,1)S(1)}, u32[]{:S(2)}, u32[]{:S(2)}) collective-permute-start(bf16[64,2048]{1,0:T(8,128)(2,1)S(1)} %get-tuple-element.40), channel_id=1, source_target_pairs={{0,2},{1,7},{2,0},{3,5},{4,6},{5,3},{6,4},{7,1},{8,10},{9,15},{10,... | collective-permute-start | bytes 786440 | tf_op jit(solution)/shard_map/ppermute | solution.py:374
  46.6 1.1 %collective-permute-done.6 = bf16[64,2048]{1,0:T(8,128)(2,1)S(1)} collective-permute-done((bf16[64,2048]{1,0:T(8,128)(2,1)S(1)}, bf16[64,2048]{1,0:T(8,128)(2,1)S(1)}, u32[]{:S(2)}, u32[]{:S(2)}) %collective-permute-start.6) | collective-permute-done | bytes 262176 | tf_op jit(solution)/shard_map/ppermute | solution.py:374
  47.7 1.9 %collective-permute-start.7 = (bf16[32,2048]{1,0:T(8,128)(2,1)S(1)}, bf16[32,2048]{1,0:T(8,128)(2,1)S(1)}, u32[]{:S(2)}, u32[]{:S(2)}) collective-permute-start(bf16[32,2048]{1,0:T(8,128)(2,1)S(1)} %slice.31), channel_id=1, source_target_pairs={{0,6},{1,3},{2,4},{3,1},{4,2},{5,7},{6,0},{7,5},{8,14},{9,11},{10,... | collective-permute-start | bytes 393224 | tf_op jit(solution)/shard_map/ppermute | solution.py:376
  49.7 0.8 %collective-permute-done.9 = bf16[64,2048]{1,0:T(8,128)(2,1)S(1)} collective-permute-done((bf16[64,2048]{1,0:T(8,128)(2,1)S(1)}, bf16[64,2048]{1,0:T(8,128)(2,1)S(1)}, u32[]{:S(2)}, u32[]{:S(2)}) %collective-permute-start.9) | collective-permute-done | bytes 262176 | tf_op jit(solution)/shard_map/ppermute | solution.py:374
  50.6 2.6 %collective-permute-start.10 = (bf16[32,2048]{1,0:T(8,128)(2,1)S(1)}, bf16[32,2048]{1,0:T(8,128)(2,1)S(1)}, u32[]{:S(2)}, u32[]{:S(2)}) collective-permute-start(bf16[32,2048]{1,0:T(8,128)(2,1)S(1)} %slice.30), channel_id=1, source_target_pairs={{0,6},{1,3},{2,4},{3,1},{4,2},{5,7},{6,0},{7,5},{8,14},{9,11},{10,... | collective-permute-start | bytes 393224 | tf_op jit(solution)/shard_map/ppermute | solution.py:376
  53.1 0.3 collective-permute-done.7
  53.5 1.9 %collective-permute-start.8 = (bf16[32,2048]{1,0:T(8,128)(2,1)S(1)}, bf16[32,2048]{1,0:T(8,128)(2,1)S(1)}, u32[]{:S(2)}, u32[]{:S(2)}) collective-permute-start(bf16[32,2048]{1,0:T(8,128)(2,1)S(1)} %fusion.1), channel_id=1, source_target_pairs={{0,8},{8,16},{16,24},{24,32},{32,40},{40,48},{48,56},{56,64},{64,7... | collective-permute-start | bytes 393224 | tf_op jit(solution)/shard_map/ppermute | solution.py:378
  55.4 0.8 %collective-permute-done.10 = bf16[32,2048]{1,0:T(8,128)(2,1)S(1)} collective-permute-done((bf16[32,2048]{1,0:T(8,128)(2,1)S(1)}, bf16[32,2048]{1,0:T(8,128)(2,1)S(1)}, u32[]{:S(2)}, u32[]{:S(2)}) %collective-permute-start.10) | collective-permute-done | bytes 131104 | tf_op jit(solution)/shard_map/ppermute | solution.py:376
  56.3 1.9 %collective-permute-start.11 = (bf16[32,2048]{1,0:T(8,128)(2,1)S(1)}, bf16[32,2048]{1,0:T(8,128)(2,1)S(1)}, u32[]{:S(2)}, u32[]{:S(2)}) collective-permute-start(bf16[32,2048]{1,0:T(8,128)(2,1)S(1)} %fusion), channel_id=1, source_target_pairs={{0,8},{8,16},{16,24},{24,32},{32,40},{40,48},{48,56},{56,64},{64,7... | collective-permute-start | bytes 393224 | tf_op jit(solution)/shard_map/ppermute | solution.py:378
  58.2 7.4 %collective-permute-done.8 = bf16[32,2048]{1,0:T(8,128)(2,1)S(1)} collective-permute-done((bf16[32,2048]{1,0:T(8,128)(2,1)S(1)}, bf16[32,2048]{1,0:T(8,128)(2,1)S(1)}, u32[]{:S(2)}, u32[]{:S(2)}) %collective-permute-start.8) | collective-permute-done | bytes 131104 | tf_op jit(solution)/shard_map/ppermute | solution.py:378
  65.6 3.8 %collective-permute-done.11 = bf16[32,2048]{1,0:T(8,128)(2,1)S(1)} collective-permute-done((bf16[32,2048]{1,0:T(8,128)(2,1)S(1)}, bf16[32,2048]{1,0:T(8,128)(2,1)S(1)}, u32[]{:S(2)}, u32[]{:S(2)}) %collective-permute-start.11) | collective-permute-done | bytes 131104 | tf_op jit(solution)/shard_map/ppermute | solution.py:378
  69.4 0.8 %maximum_convert_fusion = f32[32,4096]{1,0:T(8,128)} fusion(bf16[32,2048]{1,0:T(8,128)(2,1)S(1)} %collective-permute-done.11, bf16[32,2048]{1,0:T(8,128)(2,1)S(1)} %collective-permute-done.8), kind=kLoop, calls=%fused_computation.8 | loop fusion | flops 524288 | bytes 786432 | tf_op jit(solution)/shard_map/convert_element_type | solution.py:379
  (7 shorter events, 0.2 us)
Async XLA Ops:
  0.0 37.3 %slice-start = ((s8[8388608]{0:T(1024)(128)(4,1)}), s8[4194304]{0:T(1024)(128)(4,1)S(1)}, s32[]{:S(2)}) async-start(s8[8388608]{0:T(1024)(128)(4,1)} %bitcast.3), calls=%async_computation | async-start | bytes 8388608
  0.0 38.6 %collective-permute-start.5 = (bf16[1024,4096]{1,0:T(8,128)(2,1)}, bf16[1024,4096]{1,0:T(8,128)(2,1)S(1)}, u32[]{:S(2)}, u32[]{:S(2)}) collective-permute-start(bf16[1024,4096]{1,0:T(8,128)(2,1)} %w_ref.1), channel_id=1, source_target_pairs={{0,1},{1,0},{2,3},{3,2},{4,5},{5,4},{6,7},{7,6},{8,9},{9,8},{10,11... | collective-permute-start | bytes 25165832 | tf_op jit(solution)/shard_map/ppermute | solution.py:282
  12.6 6.1 %collective-permute-start = (bf16[768,128]{1,0:T(8,128)(2,1)}, bf16[768,128]{1,0:T(8,128)(2,1)S(1)}, u32[]{:S(2)}, u32[]{:S(2)}) collective-permute-start(bf16[768,128]{1,0:T(8,128)(2,1)} %bitcast.5), channel_id=1, source_target_pairs={{0,8},{8,16},{16,24},{24,32},{32,40},{40,48},{48,56},{56,64},{64,7... | collective-permute-start | bytes 589832 | tf_op jit(solution)/shard_map/ppermute | solution.py:253
  14.0 10.4 %collective-permute-start.2 = (bf16[768,128]{1,0:T(8,128)(2,1)}, bf16[768,128]{1,0:T(8,128)(2,1)S(1)}, u32[]{:S(2)}, u32[]{:S(2)}) collective-permute-start(bf16[768,128]{1,0:T(8,128)(2,1)} %bitcast.7), channel_id=1, source_target_pairs={{0,8},{8,16},{16,24},{24,32},{32,40},{40,48},{48,56},{56,64},{64,7... | collective-permute-start | bytes 589832 | tf_op jit(solution)/shard_map/ppermute | solution.py:253
  18.8 13.2 %collective-permute-start.1 = (bf16[768,128]{1,0:T(8,128)(2,1)S(1)}, bf16[768,128]{1,0:T(8,128)(2,1)S(1)}, u32[]{:S(2)}, u32[]{:S(2)}) collective-permute-start(bf16[768,128]{1,0:T(8,128)(2,1)S(1)} %collective-permute-done.far_k_ref), channel_id=1, source_target_pairs={{0,8},{8,16},{16,24},{24,32},{32,40},{40,48},{48,56},{56,64},{64,7... | collective-permute-start | bytes 589832 | tf_op jit(solution)/shard_map/ppermute | solution.py:253
  24.3 9.3 %collective-permute-start.3 = (bf16[768,128]{1,0:T(8,128)(2,1)S(1)}, bf16[768,128]{1,0:T(8,128)(2,1)S(1)}, u32[]{:S(2)}, u32[]{:S(2)}) collective-permute-start(bf16[768,128]{1,0:T(8,128)(2,1)S(1)} %collective-permute-done.2.far_v_ref), channel_id=1, source_target_pairs={{0,8},{8,16},{16,24},{24,32},{32,40},{40,48},{48,56},{56,64},{64,7... | collective-permute-start | bytes 589832 | tf_op jit(solution)/shard_map/ppermute | solution.py:253
  27.0 10.3 %slice-start.1 = ((s8[8388608]{0:T(1024)(128)(4,1)}), s8[4194304]{0:T(1024)(128)(4,1)S(1)}, s32[]{:S(2)}) async-start(s8[8388608]{0:T(1024)(128)(4,1)} %bitcast.3), calls=%async_computation.1 | async-start | bytes 8388608
  34.5 4.1 %collective-permute-start.4 = (bf16[128,1024]{1,0:T(8,128)(2,1)S(1)}, bf16[128,1024]{1,0:T(8,128)(2,1)S(1)}, u32[]{:S(2)}, u32[]{:S(2)}) collective-permute-start(bf16[128,1024]{1,0:T(8,128)(2,1)S(1)} %get-tuple-element.36), channel_id=1, source_target_pairs={{0,1},{1,0},{2,3},{3,2},{4,5},{5,4},{6,7},{7,6},{8,9},{9,8},{10,11... | collective-permute-start | bytes 786440 | tf_op jit(solution)/shard_map/ppermute | solution.py:346
  39.3 8.3 %collective-permute-start.6 = (bf16[64,2048]{1,0:T(8,128)(2,1)S(1)}, bf16[64,2048]{1,0:T(8,128)(2,1)S(1)}, u32[]{:S(2)}, u32[]{:S(2)}) collective-permute-start(bf16[64,2048]{1,0:T(8,128)(2,1)S(1)} %get-tuple-element.38), channel_id=1, source_target_pairs={{0,2},{1,7},{2,0},{3,5},{4,6},{5,3},{6,4},{7,1},{8,10},{9,15},{10,... | collective-permute-start | bytes 786440 | tf_op jit(solution)/shard_map/ppermute | solution.py:374
  42.0 8.5 %collective-permute-start.9 = (bf16[64,2048]{1,0:T(8,128)(2,1)S(1)}, bf16[64,2048]{1,0:T(8,128)(2,1)S(1)}, u32[]{:S(2)}, u32[]{:S(2)}) collective-permute-start(bf16[64,2048]{1,0:T(8,128)(2,1)S(1)} %get-tuple-element.40), channel_id=1, source_target_pairs={{0,2},{1,7},{2,0},{3,5},{4,6},{5,3},{6,4},{7,1},{8,10},{9,15},{10,... | collective-permute-start | bytes 786440 | tf_op jit(solution)/shard_map/ppermute | solution.py:374
  47.7 5.7 %collective-permute-start.7 = (bf16[32,2048]{1,0:T(8,128)(2,1)S(1)}, bf16[32,2048]{1,0:T(8,128)(2,1)S(1)}, u32[]{:S(2)}, u32[]{:S(2)}) collective-permute-start(bf16[32,2048]{1,0:T(8,128)(2,1)S(1)} %slice.31), channel_id=1, source_target_pairs={{0,6},{1,3},{2,4},{3,1},{4,2},{5,7},{6,0},{7,5},{8,14},{9,11},{10,... | collective-permute-start | bytes 393224 | tf_op jit(solution)/shard_map/ppermute | solution.py:376
  50.6 5.7 %collective-permute-start.10 = (bf16[32,2048]{1,0:T(8,128)(2,1)S(1)}, bf16[32,2048]{1,0:T(8,128)(2,1)S(1)}, u32[]{:S(2)}, u32[]{:S(2)}) collective-permute-start(bf16[32,2048]{1,0:T(8,128)(2,1)S(1)} %slice.30), channel_id=1, source_target_pairs={{0,6},{1,3},{2,4},{3,1},{4,2},{5,7},{6,0},{7,5},{8,14},{9,11},{10,... | collective-permute-start | bytes 393224 | tf_op jit(solution)/shard_map/ppermute | solution.py:376
  53.5 12.1 %collective-permute-start.8 = (bf16[32,2048]{1,0:T(8,128)(2,1)S(1)}, bf16[32,2048]{1,0:T(8,128)(2,1)S(1)}, u32[]{:S(2)}, u32[]{:S(2)}) collective-permute-start(bf16[32,2048]{1,0:T(8,128)(2,1)S(1)} %fusion.1), channel_id=1, source_target_pairs={{0,8},{8,16},{16,24},{24,32},{32,40},{40,48},{48,56},{56,64},{64,7... | collective-permute-start | bytes 393224 | tf_op jit(solution)/shard_map/ppermute | solution.py:378
  56.3 13.1 %collective-permute-start.11 = (bf16[32,2048]{1,0:T(8,128)(2,1)S(1)}, bf16[32,2048]{1,0:T(8,128)(2,1)S(1)}, u32[]{:S(2)}, u32[]{:S(2)}) collective-permute-start(bf16[32,2048]{1,0:T(8,128)(2,1)S(1)} %fusion), channel_id=1, source_target_pairs={{0,8},{8,16},{16,24},{24,32},{32,40},{40,48},{48,56},{56,64},{64,7... | collective-permute-start | bytes 393224 | tf_op jit(solution)/shard_map/ppermute | solution.py:378

commit v4 on v3

--- a/solution.py
+++ b/solution.py
@@ -356,10 +356,11 @@
         name="project_own",
     )(keep, out_weight)
 
-    part = out_weight.shape[1] // 2
+    width = out_weight.shape[1]
+    cut = 3 * width // 8
     size = lax.axis_size("section")
     pieces = []
-    for start in (0, part):
+    for start, part in ((0, cut), (cut, width - cut)):
         send, kept_rows = pl.pallas_call(
             functools.partial(project_kernel, start=start),
             out_shape=(jax.ShapeDtypeStruct((quarter, part), bf16), jax.ShapeDtypeStruct((quarter, part), f32)),

time: 70.9 us -> 70.6 us (level)
  waiting for transfers between devices: 17.7 us -> 16.9 us
    ppermute x2, starting transfers between devices: 4.49 us -> 5.21 us  [on_device(): second = lax.ppermute(two[eighth:].astype(bf16), 'head', chip_pairs(False))]
  transfers between devices with their start and end apart: 12 -> 12, of which waited for: 7 -> 5; matrix products, arithmetic and copies ran while one was open for 0% -> 0% of each run, Pallas kernels for 16% -> 15%
where the time goes in v4:
time: 70.6 us; the launch traced here: 70.2 us
  starting transfers between devices  40.2 us (57%)
  waiting for transfers between devices  16.9 us (24%)
  Pallas kernels  11.7 us (17%)
  other arithmetic  0.98 us (1%)
    ppermute x1, starting transfers between devices, on_device(): other_weight = lax.ppermute(out_weight, 'head', core_pairs())  12.6 us
    ppermute x2, waiting for transfers between devices, on_device(): lax.ppermute(done, 'section', [(i, (i + 1) % size) for i in range(size)])  10.7 us
    ppermute x4, starting transfers between devices, shifted(): lax.ppermute(value, axis, [(i, i + steps) for i in range(count - steps)])  9.26 us
    ppermute x2, starting transfers between devices, on_device(): first = lax.ppermute(send, 'head', chip_pairs(True))  6.49 us
    ppermute x2, starting transfers between devices, on_device(): second = lax.ppermute(two[eighth:].astype(bf16), 'head', chip_pairs(False))  5.21 us
    pallas_call x1, Pallas kernels, on_device(): pl.pallas_call(near_kernel, out_shape=(acc_shape, row_shape, row_shape),...  4.92 us
    ppermute x2, starting transfers between devices, on_device(): lax.ppermute(done, 'section', [(i, (i + 1) % size) for i in range(size)])  3.84 us
    ppermute x4, waiting for transfers between devices, shifted(): lax.ppermute(value, axis, [(i, i + steps) for i in range(count - steps)])  3.51 us
  transfers between devices with their start and end apart: 12, of which 5 were waited for; matrix products, arithmetic and copies ran while one was open for 0% of the time, Pallas kernels for 15%

profile of v4, /device:TPU:1, one launch (start us, length us, event | category | flops | bytes accessed | tf_op | source)
XLA Modules:
  0.0 70.2 jit_solution(5975974086986456247)
XLA Ops:
  0.0 0.0 slice-start
  0.0 12.6 %collective-permute-start.5 = (bf16[1024,4096]{1,0:T(8,128)(2,1)}, bf16[1024,4096]{1,0:T(8,128)(2,1)S(1)}, u32[]{:S(2)}, u32[]{:S(2)}) collective-permute-start(bf16[1024,4096]{1,0:T(8,128)(2,1)} %w_ref.1), channel_id=1, source_target_pairs={{0,1},{1,0},{2,3},{3,2},{4,5},{5,4},{6,7},{7,6},{8,9},{9,8},{10,11... | collective-permute-start | bytes 25165832 | tf_op jit(solution)/shard_map/ppermute | solution.py:282
  12.6 1.3 %collective-permute-start = (bf16[768,128]{1,0:T(8,128)(2,1)}, bf16[768,128]{1,0:T(8,128)(2,1)S(1)}, u32[]{:S(2)}, u32[]{:S(2)}) collective-permute-start(bf16[768,128]{1,0:T(8,128)(2,1)} %bitcast.5), channel_id=1, source_target_pairs={{0,8},{8,16},{16,24},{24,32},{32,40},{40,48},{48,56},{56,64},{64,7... | collective-permute-start | bytes 589832 | tf_op jit(solution)/shard_map/ppermute | solution.py:253
  14.0 1.3 %collective-permute-start.2 = (bf16[768,128]{1,0:T(8,128)(2,1)}, bf16[768,128]{1,0:T(8,128)(2,1)S(1)}, u32[]{:S(2)}, u32[]{:S(2)}) collective-permute-start(bf16[768,128]{1,0:T(8,128)(2,1)} %bitcast.7), channel_id=1, source_target_pairs={{0,8},{8,16},{16,24},{24,32},{32,40},{40,48},{48,56},{56,64},{64,7... | collective-permute-start | bytes 589832 | tf_op jit(solution)/shard_map/ppermute | solution.py:253
  15.3 3.5 %collective-permute-done.far_k_ref = bf16[768,128]{1,0:T(8,128)(2,1)S(1)} collective-permute-done((bf16[768,128]{1,0:T(8,128)(2,1)}, bf16[768,128]{1,0:T(8,128)(2,1)S(1)}, u32[]{:S(2)}, u32[]{:S(2)}) %collective-permute-start) | collective-permute-done | bytes 196640 | tf_op jit(solution)/shard_map/ppermute | solution.py:253
  18.8 4.0 %collective-permute-start.1 = (bf16[768,128]{1,0:T(8,128)(2,1)S(1)}, bf16[768,128]{1,0:T(8,128)(2,1)S(1)}, u32[]{:S(2)}, u32[]{:S(2)}) collective-permute-start(bf16[768,128]{1,0:T(8,128)(2,1)S(1)} %collective-permute-done.far_k_ref), channel_id=1, source_target_pairs={{0,8},{8,16},{16,24},{24,32},{32,40},{40,48},{48,56},{56,64},{64,7... | collective-permute-start | bytes 589832 | tf_op jit(solution)/shard_map/ppermute | solution.py:253
  22.8 1.5 %prepare.1 = (bf16[256,1024]{1,0:T(8,128)(2,1)S(1)}, s32[8,256]{1,0:T(8,128)S(1)}, f32[8,256]{1,0:T(8,128)S(1)}, bf16[256,128]{1,0:T(8,128)(2,1)S(1)}, bf16[768,...) custom-call(s32[96]{0:T(128)} %counts_hbm.1, s32[2,96]{1,0:T(2,128)} %bitcast.9, ...), custom_call_target="tpu_custom_call" | custom-call | flops 1048576 | bytes 1048576 | tf_op jit(solution)/shard_map/prepare/pallas_call | solution.py:292
  24.3 0.0 collective-permute-done.2.far_v_ref
  24.3 2.7 %collective-permute-start.3 = (bf16[768,128]{1,0:T(8,128)(2,1)S(1)}, bf16[768,128]{1,0:T(8,128)(2,1)S(1)}, u32[]{:S(2)}, u32[]{:S(2)}) collective-permute-start(bf16[768,128]{1,0:T(8,128)(2,1)S(1)} %collective-permute-done.2.far_v_ref), channel_id=1, source_target_pairs={{0,8},{8,16},{16,24},{24,32},{32,40},{40,48},{48,56},{56,64},{64,7... | collective-permute-start | bytes 589832 | tf_op jit(solution)/shard_map/ppermute | solution.py:253
  27.0 0.0 slice-start.1
  27.0 4.9 %near.1 = (f32[1024,256]{1,0:T(8,128)S(1)}, f32[8,256]{1,0:T(8,128)S(1)}, f32[8,256]{1,0:T(8,128)S(1)}) custom-call(bf16[256,1024]{1,0:T(8,128)(2,1)S(1)} %get-tuple-element.25.q_ref, s32[8,256]{1,0:T(8,128)S(1)} %get-tuple-element.23.live_ref, f32[8,256]{1,0:T(8,128)S(1)} %get-tuple-element.24.scale_ref, bf16[256,128]{1,0:T(8,128)(2,1)S(1)} %get-tuple-element.26.nk_ref, ...), custom_call_target="tpu_custom_call" | custom-call | flops 1879048192 | bytes 1048576 | tf_op jit(solution)/shard_map/near/pallas_call | solution.py:310
  31.9 0.0 collective-permute-done.1.k_ref
  31.9 1.7 %last.1 = (bf16[6144,256]{1,0:T(8,128)(2,1)S(1)}, f32[8,256]{1,0:T(8,128)S(1)}) custom-call(s32[8,256]{1,0:T(8,128)S(1)} %get-tuple-element.23.live_ref, f32[8,256]{1,0:T(8,128)S(1)} %get-tuple-element.24.scale_ref, bf16[256,1024]{1,0:T(8,128)(2,1)S(1)} %get-tuple-element.25.q_ref, bf16[256,128]{1,0:T(8,128)(2,1)S(1)} %get-tuple-element.26.nk_ref, ...), custom_call_target="tpu_custom_call" | custom-call | flops 402653184 | bytes 1048576 | tf_op jit(solution)/shard_map/last/pallas_call | solution.py:324
  33.6 0.0 collective-permute-done.3.v_ref
  33.6 0.8 %finish.1 = (bf16[128,1024]{1,0:T(8,128)(2,1)S(1)}, bf16[128,1024]{1,0:T(8,128)(2,1)S(1)}) custom-call(s32[8,256]{1,0:T(8,128)S(1)} %get-tuple-element.23.live_ref, f32[8,256]{1,0:T(8,128)S(1)} %get-tuple-element.24.scale_ref, bf16[6144,256]{1,0:T(8,128)(2,1)S(1)} %get-tuple-element.31.weights_ref, bf16[768,128]{1,0:T(8,128)(2,1)S(1)} %collective-permute-done.3.v_ref, ...), custom_call_target="tpu_custom_call" | custom-call | flops 402653184 | bytes 1048576 | tf_op jit(solution)/shard_map/finish/pallas_call | solution.py:336
  34.5 2.8 %collective-permute-start.4 = (bf16[128,1024]{1,0:T(8,128)(2,1)S(1)}, bf16[128,1024]{1,0:T(8,128)(2,1)S(1)}, u32[]{:S(2)}, u32[]{:S(2)}) collective-permute-start(bf16[128,1024]{1,0:T(8,128)(2,1)S(1)} %get-tuple-element.36), channel_id=1, source_target_pairs={{0,1},{1,0},{2,3},{3,2},{4,5},{5,4},{6,7},{7,6},{8,9},{9,8},{10,11... | collective-permute-start | bytes 786440 | tf_op jit(solution)/shard_map/ppermute | solution.py:346
  37.3 0.0 slice-done
  37.3 0.0 slice-done.1
  37.3 1.3 %project_own.1.own_ref = f32[128,4096]{1,0:T(8,128)S(1)} custom-call(bf16[128,1024]{1,0:T(8,128)(2,1)S(1)} %get-tuple-element.35.keep_ref, bf16[1024,4096]{1,0:T(8,128)(2,1)S(1)} %bitcast.4), custom_call_target="tpu_custom_call" | custom-call | flops 1073741824 | bytes 1048576 | tf_op jit(solution)/shard_map/project_own/pallas_call | solution.py:347
  38.6 0.0 collective-permute-done.4.got_ref
  38.6 0.0 collective-permute-done.5.other_w_ref
  38.6 0.9 %project.3 = (bf16[64,2560]{1,0:T(8,128)(2,1)S(1)}, f32[64,2560]{1,0:T(8,128)S(1)}) custom-call(f32[128,4096]{1,0:T(8,128)S(1)} %project_own.1.own_ref, bf16[128,1024]{1,0:T(8,128)(2,1)S(1)} %collective-permute-done.4.got_ref, bf16[1024,4096]{1,0:T(8,128)(2,1)S(1)} %collective-permute-done.5.other_w_ref), custom_call_target="tpu_custom_call" | custom-call | flops 671088640 | bytes 1048576 | tf_op jit(solution)/shard_map/project/pallas_call | solution.py:364
  39.5 1.9 %collective-permute-start.9 = (bf16[64,2560]{1,0:T(8,128)(2,1)S(1)}, bf16[64,2560]{1,0:T(8,128)(2,1)S(1)}, u32[]{:S(2)}, u32[]{:S(2)}) collective-permute-start(bf16[64,2560]{1,0:T(8,128)(2,1)S(1)} %get-tuple-element.40), channel_id=1, source_target_pairs={{0,2},{1,7},{2,0},{3,5},{4,6},{5,3},{6,4},{7,1},{8,10},{9,15},{10,... | collective-permute-start | bytes 983048 | tf_op jit(solution)/shard_map/ppermute | solution.py:375
  41.4 0.6 project.2
  42.0 4.6 %collective-permute-start.6 = (bf16[64,1536]{1,0:T(8,128)(2,1)S(1)}, bf16[64,1536]{1,0:T(8,128)(2,1)S(1)}, u32[]{:S(2)}, u32[]{:S(2)}) collective-permute-start(bf16[64,1536]{1,0:T(8,128)(2,1)S(1)} %get-tuple-element.38), channel_id=1, source_target_pairs={{0,2},{1,7},{2,0},{3,5},{4,6},{5,3},{6,4},{7,1},{8,10},{9,15},{10,... | collective-permute-start | bytes 589832 | tf_op jit(solution)/shard_map/ppermute | solution.py:375
  46.6 1.9 %collective-permute-done.9 = bf16[64,2560]{1,0:T(8,128)(2,1)S(1)} collective-permute-done((bf16[64,2560]{1,0:T(8,128)(2,1)S(1)}, bf16[64,2560]{1,0:T(8,128)(2,1)S(1)}, u32[]{:S(2)}, u32[]{:S(2)}) %collective-permute-start.9) | collective-permute-done | bytes 327712 | tf_op jit(solution)/shard_map/ppermute | solution.py:375
  48.5 0.1 convert_add_fusion
  48.6 1.9 %collective-permute-start.10 = (bf16[32,2560]{1,0:T(8,128)(2,1)S(1)}, bf16[32,2560]{1,0:T(8,128)(2,1)S(1)}, u32[]{:S(2)}, u32[]{:S(2)}) collective-permute-start(bf16[32,2560]{1,0:T(8,128)(2,1)S(1)} %slice.30), channel_id=1, source_target_pairs={{0,6},{1,3},{2,4},{3,1},{4,2},{5,7},{6,0},{7,5},{8,14},{9,11},{10,... | collective-permute-start | bytes 491528 | tf_op jit(solution)/shard_map/ppermute | solution.py:377
  50.5 0.1 collective-permute-done.6
  50.7 3.3 %collective-permute-start.7 = (bf16[32,1536]{1,0:T(8,128)(2,1)S(1)}, bf16[32,1536]{1,0:T(8,128)(2,1)S(1)}, u32[]{:S(2)}, u32[]{:S(2)}) collective-permute-start(bf16[32,1536]{1,0:T(8,128)(2,1)S(1)} %slice.31), channel_id=1, source_target_pairs={{0,6},{1,3},{2,4},{3,1},{4,2},{5,7},{6,0},{7,5},{8,14},{9,11},{10,... | collective-permute-start | bytes 294920 | tf_op jit(solution)/shard_map/ppermute | solution.py:377
  54.0 0.7 collective-permute-done.10
  54.7 1.9 %collective-permute-start.11 = (bf16[32,2560]{1,0:T(8,128)(2,1)S(1)}, bf16[32,2560]{1,0:T(8,128)(2,1)S(1)}, u32[]{:S(2)}, u32[]{:S(2)}) collective-permute-start(bf16[32,2560]{1,0:T(8,128)(2,1)S(1)} %fusion), channel_id=1, source_target_pairs={{0,8},{8,16},{16,24},{24,32},{32,40},{40,48},{48,56},{56,64},{64,7... | collective-permute-start | bytes 491528 | tf_op jit(solution)/shard_map/ppermute | solution.py:379
  56.6 0.0 collective-permute-done.7
  56.7 1.9 %collective-permute-start.8 = (bf16[32,1536]{1,0:T(8,128)(2,1)S(1)}, bf16[32,1536]{1,0:T(8,128)(2,1)S(1)}, u32[]{:S(2)}, u32[]{:S(2)}) collective-permute-start(bf16[32,1536]{1,0:T(8,128)(2,1)S(1)} %fusion.1), channel_id=1, source_target_pairs={{0,8},{8,16},{16,24},{24,32},{32,40},{40,48},{48,56},{56,64},{64,7... | collective-permute-start | bytes 294920 | tf_op jit(solution)/shard_map/ppermute | solution.py:379
  58.6 10.7 %collective-permute-done.8 = bf16[32,1536]{1,0:T(8,128)(2,1)S(1)} collective-permute-done((bf16[32,1536]{1,0:T(8,128)(2,1)S(1)}, bf16[32,1536]{1,0:T(8,128)(2,1)S(1)}, u32[]{:S(2)}, u32[]{:S(2)}) %collective-permute-start.8) | collective-permute-done | bytes 98336 | tf_op jit(solution)/shard_map/ppermute | solution.py:379
  69.3 0.0 collective-permute-done.11
  69.3 0.8 %maximum_convert_fusion = f32[32,4096]{1,0:T(8,128)} fusion(bf16[32,2560]{1,0:T(8,128)(2,1)S(1)} %collective-permute-done.11, bf16[32,1536]{1,0:T(8,128)(2,1)S(1)} %collective-permute-done.8), kind=kLoop, calls=%fused_computation.5 | loop fusion | flops 524288 | bytes 786432 | tf_op jit(solution)/shard_map/convert_element_type | solution.py:380
  (6 shorter events, 0.1 us)
Async XLA Ops:
  0.0 37.3 %slice-start = ((s8[8388608]{0:T(1024)(128)(4,1)}), s8[4194304]{0:T(1024)(128)(4,1)S(1)}, s32[]{:S(2)}) async-start(s8[8388608]{0:T(1024)(128)(4,1)} %bitcast.3), calls=%async_computation | async-start | bytes 8388608
  0.0 38.6 %collective-permute-start.5 = (bf16[1024,4096]{1,0:T(8,128)(2,1)}, bf16[1024,4096]{1,0:T(8,128)(2,1)S(1)}, u32[]{:S(2)}, u32[]{:S(2)}) collective-permute-start(bf16[1024,4096]{1,0:T(8,128)(2,1)} %w_ref.1), channel_id=1, source_target_pairs={{0,1},{1,0},{2,3},{3,2},{4,5},{5,4},{6,7},{7,6},{8,9},{9,8},{10,11... | collective-permute-start | bytes 25165832 | tf_op jit(solution)/shard_map/ppermute | solution.py:282
  12.6 6.1 %collective-permute-start = (bf16[768,128]{1,0:T(8,128)(2,1)}, bf16[768,128]{1,0:T(8,128)(2,1)S(1)}, u32[]{:S(2)}, u32[]{:S(2)}) collective-permute-start(bf16[768,128]{1,0:T(8,128)(2,1)} %bitcast.5), channel_id=1, source_target_pairs={{0,8},{8,16},{16,24},{24,32},{32,40},{40,48},{48,56},{56,64},{64,7... | collective-permute-start | bytes 589832 | tf_op jit(solution)/shard_map/ppermute | solution.py:253
  14.0 10.4 %collective-permute-start.2 = (bf16[768,128]{1,0:T(8,128)(2,1)}, bf16[768,128]{1,0:T(8,128)(2,1)S(1)}, u32[]{:S(2)}, u32[]{:S(2)}) collective-permute-start(bf16[768,128]{1,0:T(8,128)(2,1)} %bitcast.7), channel_id=1, source_target_pairs={{0,8},{8,16},{16,24},{24,32},{32,40},{40,48},{48,56},{56,64},{64,7... | collective-permute-start | bytes 589832 | tf_op jit(solution)/shard_map/ppermute | solution.py:253
  18.8 13.2 %collective-permute-start.1 = (bf16[768,128]{1,0:T(8,128)(2,1)S(1)}, bf16[768,128]{1,0:T(8,128)(2,1)S(1)}, u32[]{:S(2)}, u32[]{:S(2)}) collective-permute-start(bf16[768,128]{1,0:T(8,128)(2,1)S(1)} %collective-permute-done.far_k_ref), channel_id=1, source_target_pairs={{0,8},{8,16},{16,24},{24,32},{32,40},{40,48},{48,56},{56,64},{64,7... | collective-permute-start | bytes 589832 | tf_op jit(solution)/shard_map/ppermute | solution.py:253
  24.3 9.3 %collective-permute-start.3 = (bf16[768,128]{1,0:T(8,128)(2,1)S(1)}, bf16[768,128]{1,0:T(8,128)(2,1)S(1)}, u32[]{:S(2)}, u32[]{:S(2)}) collective-permute-start(bf16[768,128]{1,0:T(8,128)(2,1)S(1)} %collective-permute-done.2.far_v_ref), channel_id=1, source_target_pairs={{0,8},{8,16},{16,24},{24,32},{32,40},{40,48},{48,56},{56,64},{64,7... | collective-permute-start | bytes 589832 | tf_op jit(solution)/shard_map/ppermute | solution.py:253
  27.0 10.3 %slice-start.1 = ((s8[8388608]{0:T(1024)(128)(4,1)}), s8[4194304]{0:T(1024)(128)(4,1)S(1)}, s32[]{:S(2)}) async-start(s8[8388608]{0:T(1024)(128)(4,1)} %bitcast.3), calls=%async_computation.1 | async-start | bytes 8388608
  34.5 4.1 %collective-permute-start.4 = (bf16[128,1024]{1,0:T(8,128)(2,1)S(1)}, bf16[128,1024]{1,0:T(8,128)(2,1)S(1)}, u32[]{:S(2)}, u32[]{:S(2)}) collective-permute-start(bf16[128,1024]{1,0:T(8,128)(2,1)S(1)} %get-tuple-element.36), channel_id=1, source_target_pairs={{0,1},{1,0},{2,3},{3,2},{4,5},{5,4},{6,7},{7,6},{8,9},{9,8},{10,11... | collective-permute-start | bytes 786440 | tf_op jit(solution)/shard_map/ppermute | solution.py:346
  39.5 9.0 %collective-permute-start.9 = (bf16[64,2560]{1,0:T(8,128)(2,1)S(1)}, bf16[64,2560]{1,0:T(8,128)(2,1)S(1)}, u32[]{:S(2)}, u32[]{:S(2)}) collective-permute-start(bf16[64,2560]{1,0:T(8,128)(2,1)S(1)} %get-tuple-element.40), channel_id=1, source_target_pairs={{0,2},{1,7},{2,0},{3,5},{4,6},{5,3},{6,4},{7,1},{8,10},{9,15},{10,... | collective-permute-start | bytes 983048 | tf_op jit(solution)/shard_map/ppermute | solution.py:375
  42.0 8.6 %collective-permute-start.6 = (bf16[64,1536]{1,0:T(8,128)(2,1)S(1)}, bf16[64,1536]{1,0:T(8,128)(2,1)S(1)}, u32[]{:S(2)}, u32[]{:S(2)}) collective-permute-start(bf16[64,1536]{1,0:T(8,128)(2,1)S(1)} %get-tuple-element.38), channel_id=1, source_target_pairs={{0,2},{1,7},{2,0},{3,5},{4,6},{5,3},{6,4},{7,1},{8,10},{9,15},{10,... | collective-permute-start | bytes 589832 | tf_op jit(solution)/shard_map/ppermute | solution.py:375
  48.6 6.1 %collective-permute-start.10 = (bf16[32,2560]{1,0:T(8,128)(2,1)S(1)}, bf16[32,2560]{1,0:T(8,128)(2,1)S(1)}, u32[]{:S(2)}, u32[]{:S(2)}) collective-permute-start(bf16[32,2560]{1,0:T(8,128)(2,1)S(1)} %slice.30), channel_id=1, source_target_pairs={{0,6},{1,3},{2,4},{3,1},{4,2},{5,7},{6,0},{7,5},{8,14},{9,11},{10,... | collective-permute-start | bytes 491528 | tf_op jit(solution)/shard_map/ppermute | solution.py:377
  50.7 6.0 %collective-permute-start.7 = (bf16[32,1536]{1,0:T(8,128)(2,1)S(1)}, bf16[32,1536]{1,0:T(8,128)(2,1)S(1)}, u32[]{:S(2)}, u32[]{:S(2)}) collective-permute-start(bf16[32,1536]{1,0:T(8,128)(2,1)S(1)} %slice.31), channel_id=1, source_target_pairs={{0,6},{1,3},{2,4},{3,1},{4,2},{5,7},{6,0},{7,5},{8,14},{9,11},{10,... | collective-permute-start | bytes 294920 | tf_op jit(solution)/shard_map/ppermute | solution.py:377
  54.7 14.6 %collective-permute-start.11 = (bf16[32,2560]{1,0:T(8,128)(2,1)S(1)}, bf16[32,2560]{1,0:T(8,128)(2,1)S(1)}, u32[]{:S(2)}, u32[]{:S(2)}) collective-permute-start(bf16[32,2560]{1,0:T(8,128)(2,1)S(1)} %fusion), channel_id=1, source_target_pairs={{0,8},{8,16},{16,24},{24,32},{32,40},{40,48},{48,56},{56,64},{64,7... | collective-permute-start | bytes 491528 | tf_op jit(solution)/shard_map/ppermute | solution.py:379
  56.7 12.6 %collective-permute-start.8 = (bf16[32,1536]{1,0:T(8,128)(2,1)S(1)}, bf16[32,1536]{1,0:T(8,128)(2,1)S(1)}, u32[]{:S(2)}, u32[]{:S(2)}) collective-permute-start(bf16[32,1536]{1,0:T(8,128)(2,1)S(1)} %fusion.1), channel_id=1, source_target_pairs={{0,8},{8,16},{16,24},{24,32},{32,40},{40,48},{48,56},{56,64},{64,7... | collective-permute-start | bytes 294920 | tf_op jit(solution)/shard_map/ppermute | solution.py:379
